TPU v7x, 256 devices: a whole 4x4x8 slice. The times are simulated.
256 devices in a mesh: temporal: 8 (over z_lo, core), spatial: 16 (over y, x), head: 2 (over z_hi).
Axes of the slice: x: 4, y: 4, z: 8 (z_hi: 2, z_lo: 4; z = z_hi * 4 + z_lo), core: 2. Of those that a mesh axis runs over, the one named last changes fastest.
Arguments:
- queries: bfloat16 [32768, 2048], P(('temporal', 'spatial'), 'head'), may hold values from -120 to 120
- keys: bfloat16 [32768, 2048], P(('temporal', 'spatial'), 'head'), may hold values from -6 to 6
- values: bfloat16 [32768, 2048], P(('temporal', 'spatial'), 'head'), may hold values from -6 to 6
- window: int32 [8, 1, 16, 27], P('temporal', None, 'spatial'), may hold values from 0 to 1, as said below
Outputs:
- attended: bfloat16 [32768, 2048], P(('temporal', 'spatial'), 'head')
Inputs may be any that keep to these rules, and one draw needn't show every extreme that they name: `window`: entry 9 (dt + 1) + 3 (dh + 1) + (dw + 1) of a tile's pattern admits the key tile at offset (dt, dh, dw) in tiles along frames, rows and columns; entry 13 is 1 for every tile.
All inputs are finite; a program needn't handle non-finite values.
Results may differ from a plain program's by a relative error of at most 0.0028.
Values may be sent and summed in bfloat16 or wider, within the bound.
No kernel may reach another device: no remote copies, remote signals or barrier semaphores. Data moves between devices by JAX's collectives and lax.ppermute only.
A program may use at most 64 MiB of HBM per device.

v0:
```python
import math

import jax
import jax.numpy as jnp
from jax import lax
from jax.sharding import PartitionSpec as P

D_HEAD = 128
TILE_T = 4
TILE_H = 8
TILE_W = 8


def with_halo(array, sides, width):
    for axis, dim in sides:
        peers, length = (lax.axis_size(axis), array.shape[dim])
        up = [(i, (i + 1) % peers) for i in range(peers - 1)]
        down = [(j, i) for i, j in up]
        last = lax.slice_in_dim(array, length - width, length, axis=dim)
        initial = lax.slice_in_dim(array, 0, width, axis=dim)
        before = lax.ppermute(last, axis, up)
        after = lax.ppermute(initial, axis, down)
        array = jnp.concatenate([before, array, after], axis=dim)
    return array


def tile_mask(pattern, tile_row, first_row, window_rows, time_ok, width_ok):
    height_step = first_row - tile_row
    picked = [pattern[:, height_step + 1, :] == 1]
    chosen = jnp.stack(picked, axis=1)
    allowed = chosen & time_ok[:, None, None] & width_ok[None, None, :]
    return jnp.broadcast_to(
        allowed[:, None, :, None, :, None], (3, TILE_T, window_rows, TILE_H, 3, TILE_W)
    ).reshape(-1)


def attend(query_tile, key_window, value_window, key_ok):
    heads_here = query_tile.shape[1]
    group = min(2, heads_here)
    scale = 1.0 / math.sqrt(D_HEAD)
    pieces = []
    for head_start in range(0, heads_here, group):
        query_part = query_tile[:, head_start : head_start + group]
        key_part = key_window[:, head_start : head_start + group]
        value_part = value_window[:, head_start : head_start + group]
        scores = (
            jnp.einsum("qhd,khd->hqk", query_part, key_part, preferred_element_type=jnp.float32)
            * scale
        )
        scores = jnp.where(key_ok[None, None, :], scores, -jnp.inf)
        peak = jnp.max(scores, axis=-1, keepdims=True)
        weights = jnp.exp(scores - peak)
        total = jnp.sum(weights, axis=-1)
        attended_part = jnp.einsum(
            "hqk,khd->qhd",
            weights.astype(jnp.bfloat16),
            value_part,
            preferred_element_type=jnp.float32,
        )
        attended_part = attended_part / jnp.transpose(total)[:, :, None]
        pieces.append(attended_part.astype(jnp.bfloat16).reshape(attended_part.shape[0], -1))
    return jnp.concatenate(pieces, axis=1)


def body(queries, keys, values, window):
    space_count = lax.axis_size("spatial")
    time_count = lax.axis_size("temporal")
    tokens_dev, channels = queries.shape
    tile_rows = window.shape[1]
    height = tile_rows * TILE_H
    shard_rows = tokens_dev // (space_count * TILE_W)
    split = 1
    groups = space_count // split
    span = split * TILE_W
    part_channels = channels // split

    def to_blocks(tensor):
        shaped = tensor.reshape(shard_rows, groups, span, split, part_channels)
        return jnp.transpose(shaped, (3, 1, 0, 2, 4)).reshape(
            space_count, shard_rows, span, part_channels
        )

    def from_blocks(tensor):
        return tensor.reshape(TILE_T, height, span, part_channels)

    query_block, key_block, value_block = (
        lax.all_to_all(to_blocks(queries), "spatial", split_axis=0, concat_axis=0, tiled=True),
        lax.all_to_all(to_blocks(keys), "spatial", split_axis=0, concat_axis=0, tiled=True),
        lax.all_to_all(to_blocks(values), "spatial", split_axis=0, concat_axis=0, tiled=True),
    )
    add_key_block = from_blocks(key_block)
    add_value_block = from_blocks(value_block)
    paired = jnp.stack([add_key_block, add_value_block]).reshape(
        2, 1, TILE_T, height, split, TILE_W, part_channels
    )
    padded = with_halo(paired, (("temporal", 1), ("spatial", 4)), 1)
    query_block = from_blocks(query_block)
    column_base = lax.axis_index("spatial")
    offsets = jnp.arange(3, dtype=jnp.int32) - 1
    time_index = lax.axis_index("temporal") + offsets
    time_ok = (time_index >= 0) & (time_index < time_count)
    window_rows = min(3, tile_rows)
    heads_here = part_channels // D_HEAD
    width_index = column_base + 0 + offsets
    width_ok = (width_index >= 0) & (width_index < space_count)
    pattern_column = lax.dynamic_index_in_dim(window, 0, 2, keepdims=False)
    pattern_rows = pattern_column.reshape(tile_rows, 3, 3, 3)
    first_row = min(max(0 - 1, 0), tile_rows - window_rows)
    key_ok = tile_mask(pattern_rows[0], 0, first_row, window_rows, time_ok, width_ok)
    query_tile = query_block.reshape(-1, heads_here, D_HEAD)
    row_low = first_row * TILE_H
    row_high = row_low + window_rows * TILE_H
    key_window = padded[0, :, :, row_low:row_high, 0:3].reshape(-1, heads_here, D_HEAD)
    value_window = padded[1, :, :, row_low:row_high, 0:3].reshape(-1, heads_here, D_HEAD)
    attended_tile = attend(query_tile, key_window, value_window, key_ok)
    outputs = attended_tile.reshape(TILE_T, TILE_H, TILE_W, part_channels)
    result = outputs.reshape(space_count, shard_rows, span, part_channels)
    returned = lax.all_to_all(result, "spatial", split_axis=0, concat_axis=0, tiled=True)
    shaped = returned.reshape(split, groups, shard_rows, span, part_channels)
    return jnp.transpose(shaped, (2, 1, 3, 0, 4)).reshape(tokens_dev, channels)


def solution(mesh):
    return jax.shard_map(
        body,
        mesh=mesh,
        in_specs=(
            P(("temporal", "spatial"), "head"),
            P(("temporal", "spatial"), "head"),
            P(("temporal", "spatial"), "head"),
            P("temporal", None, "spatial", None),
        ),
        out_specs=P(("temporal", "spatial"), "head"),
        check_vma=False,
    )
```

profile of v0, /device:TPU:32, one launch (start us, length us, event | category | flops | bytes accessed | tf_op | source)
XLA Modules:
  0.0 206.3 jit_solution(6049671225009089213)
XLA Ops:
  0.0 1.9 copy.153
  1.9 7.0 %all-to-all-start = ((bf16[16,2,8,1024]{3,2,1,0:T(8,128)(2,1)}), bf16[16,2,8,1024]{3,2,1,0:T(8,128)(2,1)S(1)}, u32[]{:S(2)}, u32[]{:S(2)}) async-start(bf16[16,2,8,1024]{3,2,1,0:T(8,128)(2,1)} %bitcast.77), calls=%async_computation | async-start | bytes 1048576 | tf_op jit(solution)/shard_map/all_to_all | solution.py:88
  8.9 1.1 copy.152
  10.0 10.4 %all-to-all-done = bf16[16,2,8,1024]{3,2,1,0:T(8,128)(2,1)S(1)} async-done(((bf16[16,2,8,1024]{3,2,1,0:T(8,128)(2,1)}), bf16[16,2,8,1024]{3,2,1,0:T(8,128)(2,1)S(1)}, u32[]{:S(2)}, u32[]{:S(2)}) %all-to-all-start) | async-done | bytes 524320 | tf_op jit(solution)/shard_map/all_to_all | solution.py:88
  20.5 13.8 %all_to_all.20 = bf16[16,2,8,1024]{3,2,1,0:T(8,128)(2,1)S(1)} all-to-all(bf16[16,2,8,1024]{3,2,1,0:T(8,128)(2,1)S(1)} %bitcast.86), channel_id=1, replica_groups=mesh['temporal'=8,'spatial'=16,'head'=2] {'spatial'}, dimensions={0} | all-to-all | bytes 1048576 | tf_op jit(solution)/shard_map/all_to_all | solution.py:89
  34.4 2.1 collective-permute-start
  36.5 3.6 %collective-permute-start.1 = (bf16[2,1,4,8,1,8,1024]{6,5,3,2,0,4,1:T(8,128)(2,1)S(1)}, bf16[2,1,4,8,1,8,1024]{6,5,3,2,0,4,1:T(8,128)(2,1)S(1)}, u32[]{:S(2)}, u32[]{:S(2)}) collective-permute-start(bf16[2,1,4,8,1,8,1024]{6,5,3,2,0,4,1:T(8,128)(2,1)S(1)} %maximum_bitcast_fusion), channel_id=1, source_target_pairs={{32,0},{64,32},{96,64},{128,96},{160,128},{192,160},{224,192},{33,... | collective-permute-start | bytes 3145736 | tf_op jit(solution)/shard_map/ppermute | solution.py:22
  40.1 10.5 %collective-permute-done = bf16[2,1,4,8,1,8,1024]{6,5,3,2,0,4,1:T(8,128)(2,1)S(1)} collective-permute-done((bf16[2,1,4,8,1,8,1024]{6,5,3,2,0,4,1:T(8,128)(2,1)S(1)}, bf16[2,1,4,8,1,8,1024]{6,5,3,2,0,4,1:T(8,128)(2,1)S(1)}, u32[]{:S(2)}, u32[]{:S(2)}) %collective-permute-start) | collective-permute-done | bytes 1048608 | tf_op jit(solution)/shard_map/ppermute | solution.py:21
  50.7 1.8 collective-permute-done.1
  52.4 2.0 pad_maximum_fusion.1
  54.4 2.7 %collective-permute-start.2 = (bf16[2,3,4,8,1,8,1024]{6,5,3,2,0,4,1:T(8,128)(2,1)}, bf16[2,3,4,8,1,8,1024]{6,5,3,2,0,4,1:T(8,128)(2,1)S(1)}, u32[]{:S(2)}, u32[]{:S(2)}) collective-permute-start(bf16[2,3,4,8,1,8,1024]{6,5,3,2,0,4,1:T(8,128)(2,1)} %pad_maximum_fusion.1), channel_id=1, source_target_pairs={{0,2},{2,4},{4,6},{6,8},{8,10},{10,12},{12,14},{14,16},{16,18},{18... | collective-permute-start | bytes 9437192 | tf_op jit(solution)/shard_map/ppermute | solution.py:21
  57.1 1.3 collective-permute-start.3
  58.5 0.8 copy.151
  59.3 6.2 %all-to-all-start.2 = ((bf16[16,2,8,1024]{3,2,1,0:T(8,128)(2,1)}), bf16[16,2,8,1024]{3,2,1,0:T(8,128)(2,1)}, u32[]{:S(2)}, u32[]{:S(2)}) async-start(bf16[16,2,8,1024]{3,2,1,0:T(8,128)(2,1)} %bitcast.85), calls=%async_computation.2 | async-start | bytes 1048576 | tf_op jit(solution)/shard_map/all_to_all | solution.py:87
  65.5 0.5 broadcast.100
  66.1 0.6 reduce.3
  67.0 0.1 broadcast_in_dim.46
  67.1 68.5 %all-to-all-done.2 = bf16[16,2,8,1024]{3,2,1,0:T(8,128)(2,1)} async-done(((bf16[16,2,8,1024]{3,2,1,0:T(8,128)(2,1)}), bf16[16,2,8,1024]{3,2,1,0:T(8,128)(2,1)}, u32[]{:S(2)}, u32[]{:S(2)}) %all-to-all-start.2) | async-done | bytes 524320 | tf_op jit(solution)/shard_map/all_to_all | solution.py:87
  135.6 1.1 copy.82
  136.7 1.1 fusion.103
  137.9 1.7 copy-done.3
  139.6 4.7 %pad_maximum_fusion = bf16[2,3,4,8,3,8,1024]{6,5,3,2,0,4,1:T(8,128)(2,1)S(1)} fusion(bf16[2,3,4,8,1,8,1024]{6,5,3,2,0,4,1:T(8,128)(2,1)} %collective-permute-done.3, bf16[2,1,4,8,1,8,1024]{6,5,3,2,0,4,1:T(8,128)(2,1)} %copy-done.2, bf16[2,1,4,8,1,8,1024]{6,5,3,2,0,4,1:T(8,128)(2,1)} %copy-done, bf16[2,1,4,8,1,8,1024]{6,5,3,2,0,4,1:T(8,128)(2,1)} %copy-done.1, ...), kind=kLoop, calls=%fused_computation | loop fusion | flops 18874368 | bytes 18874368 | tf_op jit(solution)/shard_map/concatenate | solution.py:23
  144.2 4.7 %fusion.100 = (bf16[1,3,4,8,3,8,1024]{6,5,3,2,0,4,1:T(8,128)(2,1)}, bf16[1,3,4,8,3,8,1024]{6,5,3,2,0,4,1:T(8,128)(2,1)}) fusion(bf16[2,3,4,8,3,8,1024]{6,5,3,2,0,4,1:T(8,128)(2,1)S(1)} %pad_maximum_fusion), kind=kLoop, calls=%fused_computation.68 | loop fusion | bytes 18874368 | tf_op jit(solution)/shard_map/slice | solution.py:114
  149.0 2.8 %copy.41 = bf16[1,3,4,8,3,8,1024]{6,5,4,3,2,1,0:T(8,128)(2,1)S(1)} copy(bf16[1,3,4,8,3,8,1024]{6,5,3,2,0,4,1:T(8,128)(2,1)} %get-tuple-element.6) | data formatting | bytes 9437184 | tf_op jit(solution)/shard_map/slice | solution.py:113
  151.8 1.3 copy.81
  153.1 4.6 %fusion.102 = (bf16[2304,2,128]{2,1,0:T(2,128)(2,1)S(1)}, bf16[2304,2,128]{2,1,0:T(2,128)(2,1)}, bf16[2304,2,128]{2,1,0:T(2,128)(2,1)}, bf16[2304,2,128]{2,1,0:T(2,128)(2,1)}) fusion(bf16[2304,8,128]{2,1,0:T(8,128)(2,1)S(1)} %bitcast.79), kind=kLoop, calls=%fused_computation.70 | loop fusion | bytes 9437184 | tf_op jit(solution)/shard_map/slice | solution.py:44
  157.7 0.7 copy.39
  158.4 1.2 copy.80
  159.7 3.4 %fusion.101 = (bf16[2304,2,128]{2,1,0:T(2,128)(2,1)S(1)}, bf16[2304,2,128]{2,1,0:T(2,128)(2,1)S(1)}, bf16[2304,2,128]{2,1,0:T(2,128)(2,1)S(1)}, bf16[2304,2,128]{2,1,0:T(2,128)(2,1)S(1)}) fusion(bf16[2304,8,128]{2,1,0:T(8,128)(2,1)S(1)} %bitcast.80), kind=kLoop, calls=%fused_computation.69 | loop fusion | bytes 9437184 | tf_op jit(solution)/shard_map/slice | solution.py:45
  163.1 0.8 fusion.107
  163.9 0.6 fusion.8
  164.6 1.6 fusion.91
  166.2 1.7 copy.46
  167.8 1.7 concatenate.20
  169.5 2.9 %fusion.106 = (f32[2,256]{1,0:T(2,128)S(1)}, f32[2,256,2304]{1,2,0:T(8,128)S(1)}) fusion(bf16[256,2,128]{2,1,0:T(2,128)(2,1)} %get-tuple-element.17, bf16[2304,2,128]{2,1,0:T(2,128)(2,1)} %get-tuple-element.13, pred[2304]{0:T(1024)(128)(4,1)S(1)} %broadcast_in_dim.46), kind=kOutput, calls=%fused_computation.74 | convolution fusion | flops 305528320 | bytes 6033664 | tf_op jit(solution)/shard_map/qhd,khd->hqk/dot_general | solution.py:47
  172.4 0.6 fusion.10
  173.1 1.6 fusion.81
  174.6 1.0 copy.51
  175.7 0.7 concatenate.21
  176.4 2.7 %fusion.105 = (f32[2,256]{1,0:T(2,128)S(1)}, f32[2,256,2304]{1,2,0:T(8,128)S(1)}) fusion(bf16[256,2,128]{2,1,0:T(2,128)(2,1)} %get-tuple-element.16, bf16[2304,2,128]{2,1,0:T(2,128)(2,1)} %get-tuple-element.12, pred[2304]{0:T(1024)(128)(4,1)S(1)} %broadcast_in_dim.46), kind=kOutput, calls=%fused_computation.73 | convolution fusion | flops 305528320 | bytes 6033664 | tf_op jit(solution)/shard_map/qhd,khd->hqk/dot_general | solution.py:47
  179.2 0.6 fusion.12
  179.8 1.6 fusion.71
  181.4 1.0 copy.56
  182.5 1.7 fusion.104
  184.3 0.6 fusion.14
  184.9 0.9 fusion.61
  186.2 19.3 %all_to_all.21 = bf16[16,2,8,1024]{3,2,1,0:T(8,128)(2,1)S(1)} all-to-all(bf16[16,2,8,1024]{3,2,1,0:T(8,128)(2,1)S(1)} %pad_maximum_fusion.2), channel_id=1, replica_groups=mesh['temporal'=8,'spatial'=16,'head'=2] {'spatial'}, dimensions={0} | all-to-all | bytes 1048576 | tf_op jit(solution)/shard_map/all_to_all | solution.py:118
  205.5 0.8 copy.62
  (36 shorter events, 0.8 us)
Async XLA Ops:
  1.9 18.6 %all-to-all-start = ((bf16[16,2,8,1024]{3,2,1,0:T(8,128)(2,1)}), bf16[16,2,8,1024]{3,2,1,0:T(8,128)(2,1)S(1)}, u32[]{:S(2)}, u32[]{:S(2)}) async-start(bf16[16,2,8,1024]{3,2,1,0:T(8,128)(2,1)} %bitcast.77), calls=%async_computation | async-start | bytes 1048576 | tf_op jit(solution)/shard_map/all_to_all | solution.py:88
  20.5 38.0 %copy-start.5 = (bf16[256,1024]{1,0:T(8,128)(2,1)S(1)}, bf16[256,1024]{1,0:T(8,128)(2,1)}, u32[]{:S(2)}) copy-start(bf16[256,1024]{1,0:T(8,128)(2,1)} %param.4) | copy-start | bytes 1572868
  34.4 18.0 %copy-start = (bf16[2,1,4,8,1,8,1024]{6,5,3,2,0,4,1:T(8,128)(2,1)}, bf16[2,1,4,8,1,8,1024]{6,5,3,2,0,4,1:T(8,128)(2,1)S(1)}, u32[]{:S(2)}) copy-start(bf16[2,1,4,8,1,8,1024]{6,5,3,2,0,4,1:T(8,128)(2,1)S(1)} %maximum_bitcast_fusion) | copy-start | bytes 3145732
  34.4 31.7 %copy-start.9 = (s32[1,1,1,27]{3,2,1,0:T(1,128)S(1)}, s32[1,1,1,27]{3,2,1,0:T(1,128)}, u32[]{:S(2)}) copy-start(s32[1,1,1,27]{3,2,1,0:T(1,128)} %param.7) | copy-start | bytes 328
  34.4 16.2 %collective-permute-start = (bf16[2,1,4,8,1,8,1024]{6,5,3,2,0,4,1:T(8,128)(2,1)S(1)}, bf16[2,1,4,8,1,8,1024]{6,5,3,2,0,4,1:T(8,128)(2,1)S(1)}, u32[]{:S(2)}, u32[]{:S(2)}) collective-permute-start(bf16[2,1,4,8,1,8,1024]{6,5,3,2,0,4,1:T(8,128)(2,1)S(1)} %maximum_bitcast_fusion), channel_id=1, source_target_pairs={{0,32},{32,64},{64,96},{96,128},{128,160},{160,192},{192,224},{1,3... | collective-permute-start | bytes 3145736 | tf_op jit(solution)/shard_map/ppermute | solution.py:21
  36.5 15.9 %collective-permute-start.1 = (bf16[2,1,4,8,1,8,1024]{6,5,3,2,0,4,1:T(8,128)(2,1)S(1)}, bf16[2,1,4,8,1,8,1024]{6,5,3,2,0,4,1:T(8,128)(2,1)S(1)}, u32[]{:S(2)}, u32[]{:S(2)}) collective-permute-start(bf16[2,1,4,8,1,8,1024]{6,5,3,2,0,4,1:T(8,128)(2,1)S(1)} %maximum_bitcast_fusion), channel_id=1, source_target_pairs={{32,0},{64,32},{96,64},{128,96},{160,128},{192,160},{224,192},{33,... | collective-permute-start | bytes 3145736 | tf_op jit(solution)/shard_map/ppermute | solution.py:22
  50.6 3.8 %copy-start.1 = (bf16[2,1,4,8,1,8,1024]{6,5,3,2,0,4,1:T(8,128)(2,1)}, bf16[2,1,4,8,1,8,1024]{6,5,3,2,0,4,1:T(8,128)(2,1)S(1)}, u32[]{:S(2)}) copy-start(bf16[2,1,4,8,1,8,1024]{6,5,3,2,0,4,1:T(8,128)(2,1)S(1)} %collective-permute-done) | copy-start | bytes 3145732
  52.4 4.7 %copy-start.2 = (bf16[2,1,4,8,1,8,1024]{6,5,3,2,0,4,1:T(8,128)(2,1)}, bf16[2,1,4,8,1,8,1024]{6,5,3,2,0,4,1:T(8,128)(2,1)S(1)}, u32[]{:S(2)}) copy-start(bf16[2,1,4,8,1,8,1024]{6,5,3,2,0,4,1:T(8,128)(2,1)S(1)} %collective-permute-done.1) | copy-start | bytes 3145732
  54.4 83.4 %collective-permute-start.2 = (bf16[2,3,4,8,1,8,1024]{6,5,3,2,0,4,1:T(8,128)(2,1)}, bf16[2,3,4,8,1,8,1024]{6,5,3,2,0,4,1:T(8,128)(2,1)S(1)}, u32[]{:S(2)}, u32[]{:S(2)}) collective-permute-start(bf16[2,3,4,8,1,8,1024]{6,5,3,2,0,4,1:T(8,128)(2,1)} %pad_maximum_fusion.1), channel_id=1, source_target_pairs={{0,2},{2,4},{4,6},{6,8},{8,10},{10,12},{12,14},{14,16},{16,18},{18... | collective-permute-start | bytes 9437192 | tf_op jit(solution)/shard_map/ppermute | solution.py:21
  57.1 82.4 %collective-permute-start.3 = (bf16[2,3,4,8,1,8,1024]{6,5,3,2,0,4,1:T(8,128)(2,1)}, bf16[2,3,4,8,1,8,1024]{6,5,3,2,0,4,1:T(8,128)(2,1)}, u32[]{:S(2)}, u32[]{:S(2)}) collective-permute-start(bf16[2,3,4,8,1,8,1024]{6,5,3,2,0,4,1:T(8,128)(2,1)} %pad_maximum_fusion.1), channel_id=1, source_target_pairs={{2,0},{4,2},{6,4},{8,6},{10,8},{12,10},{14,12},{16,14},{18,16},{20... | collective-permute-start | bytes 9437192 | tf_op jit(solution)/shard_map/ppermute | solution.py:22
  59.3 76.3 %all-to-all-start.2 = ((bf16[16,2,8,1024]{3,2,1,0:T(8,128)(2,1)}), bf16[16,2,8,1024]{3,2,1,0:T(8,128)(2,1)}, u32[]{:S(2)}, u32[]{:S(2)}) async-start(bf16[16,2,8,1024]{3,2,1,0:T(8,128)(2,1)} %bitcast.85), calls=%async_computation.2 | async-start | bytes 1048576 | tf_op jit(solution)/shard_map/all_to_all | solution.py:87
  137.9 1.7 copy-start.3
  151.8 5.9 %slice-start = ((s8[4718592]{0:T(1024)(128)(4,1)}), s8[4194304]{0:T(1024)(128)(4,1)S(1)}, s32[]{:S(2)}) async-start(s8[4718592]{0:T(1024)(128)(4,1)} %bitcast.83), calls=%async_computation.4 | async-start | bytes 8388608
  153.1 4.6 %slice-start.1 = ((s8[4718592]{0:T(1024)(128)(4,1)}), s8[524288]{0:T(1024)(128)(4,1)S(1)}, s32[]{:S(2)}) async-start(s8[4718592]{0:T(1024)(128)(4,1)} %bitcast.83), calls=%async_computation.5 | async-start | bytes 1048576
  159.7 3.4 %copy-start.8 = (bf16[256,2,128]{2,1,0:T(2,128)(2,1)S(1)}, bf16[256,2,128]{2,1,0:T(2,128)(2,1)}, u32[]{:S(2)}) copy-start(bf16[256,2,128]{2,1,0:T(2,128)(2,1)} %get-tuple-element.15) | copy-start | bytes 393220
  179.2 3.4 %copy-start.4 = (bf16[2304,2,128]{2,1,0:T(2,128)(2,1)S(1)}, bf16[2304,2,128]{2,1,0:T(2,128)(2,1)}, u32[]{:S(2)}) copy-start(bf16[2304,2,128]{2,1,0:T(2,128)(2,1)} %get-tuple-element.14) | copy-start | bytes 3538948
  184.3 1.8 copy-start.6
  184.3 1.8 copy-start.7
where the time goes:
time: 208 us; the launch traced here: 206 us
  waiting for transfers between devices  91.2 us (44%)
  local copies, waits for them, and re-layouts  34.7 us (17%)
  blocking collectives  33.2 us (16%)
  starting transfers between devices  23 us (11%)
  matrix products  13.9 us (7%)
  other arithmetic  10.1 us (5%)
    all_to_all x1, waiting for transfers between devices, body(): lax.all_to_all(to_blocks(queries), 'spatial', split_axis=0, concat_axis=0...  68.5 us
    all_to_all x1, blocking collectives, body(): lax.all_to_all(result, 'spatial', split_axis=0, concat_axis=0, tiled=True)  19.3 us
    all_to_all x1, blocking collectives, body(): lax.all_to_all(to_blocks(values), 'spatial', split_axis=0, concat_axis=0,...  13.8 us
    ppermute x2, waiting for transfers between devices, with_halo(): before = lax.ppermute(last, axis, up)  10.5 us
    all_to_all x1, waiting for transfers between devices, body(): lax.all_to_all(to_blocks(keys), 'spatial', split_axis=0, concat_axis=0, t...  10.4 us
    dot_general x4, matrix products, attend(): jnp.einsum('qhd,khd->hqk', query_part, key_part, preferred_element_type=j...  8.17 us
    all_to_all x1, starting transfers between devices, body(): lax.all_to_all(to_blocks(keys), 'spatial', split_axis=0, concat_axis=0, t...  7.03 us
    concatenate x2, other arithmetic, with_halo(): array = jnp.concatenate([before, array, after], axis=dim)  6.68 us
  transfers between devices with their start and end apart: 6, of which 4 were waited for; matrix products, arithmetic and copies ran while one was open for 3% of the time, Pallas kernels for 0%

commit v1 on v0

v1 whole, which is shorter than its diff:
```python
import math

import jax
import jax.numpy as jnp
from jax import lax
from jax.experimental import pallas as pl
from jax.experimental.pallas import tpu as pltpu
from jax.sharding import PartitionSpec as P

D = 128
HEADS = 8
TILES = 8
COLS = 16
HALO = 9
BIG = 3.0e38
SCALE = math.log2(math.e) / math.sqrt(D)


def pack_kernel(q_ref, k_ref, v_ref, w_ref, kv_out, q_out):
    pattern = w_ref[...].astype(jnp.float32)
    rows = lax.broadcasted_iota(jnp.int32, (16, 128), 0)
    lanes = lax.broadcasted_iota(jnp.int32, (16, 128), 1)
    pick = 9 * (rows // 3) + 3 + rows % 3
    kept = jnp.where(lanes == pick, jnp.broadcast_to(pattern, (16, 128)), 0.0)
    marks = jnp.broadcast_to(jnp.sum(kept, axis=1, keepdims=True), (16, 128))
    low = marks[0:8].astype(jnp.bfloat16)
    high = marks[8:16].astype(jnp.bfloat16)
    for h in range(HEADS):
        lane = pl.ds(h * D, D)
        for half in range(2):
            d = 2 * h + half
            for r in range(2):
                kv_out[d, 0:HALO, r] = k_ref[r, pl.ds(7 * half, HALO), :, lane]
                kv_out[d, HALO : 2 * HALO, r] = v_ref[r, pl.ds(7 * half, HALO), :, lane]
                q_out[d, 0:TILES, r] = q_ref[r, pl.ds(8 * half, TILES), :, lane]
            q_out[d, TILES, 0] = low
            q_out[d, TILES, 1] = high


def pack(q, k, v, window):
    shaped = [x.reshape(2, COLS, 8, HEADS * D) for x in (q, k, v)]
    pattern = jnp.pad(window.reshape(1, 27), ((0, 0), (0, 101)))
    vmem = pl.BlockSpec(memory_space=pltpu.VMEM)
    return pl.pallas_call(
        pack_kernel,
        out_shape=(
            jax.ShapeDtypeStruct((16, 2 * HALO, 2, 8, D), jnp.bfloat16),
            jax.ShapeDtypeStruct((16, TILES + 1, 2, 8, D), jnp.bfloat16),
        ),
        in_specs=[vmem] * 4,
        out_specs=(vmem, vmem),
        name="pack",
    )(*shaped, pattern)


def attend_kernel(q_ref, prev_ref, own_ref, next_ref, o_ref, s_ref):
    t = lax.axis_index("temporal")
    half = lax.axis_index("spatial") % 2

    def tile(w, carry):
        q = q_ref[:, w].reshape(256, D)
        marks = q_ref[half * TILES + w, TILES].astype(jnp.float32)
        column = half * TILES + w
        tops, oks = [], []
        for a, ref in enumerate((prev_ref, own_ref, next_ref)):
            t_ok = (t + a - 1 >= 0) & (t + a - 1 < 8)
            for b in range(3):
                w_ok = (column + b - 1 >= 0) & (column + b - 1 < COLS)
                index = jnp.clip(w + b - 1 + half, 0, HALO - 1)
                j = 3 * a + b
                k = ref[:, index].reshape(256, D)
                s = lax.dot_general(
                    q, k, (((1,), (1,)), ((), ())), preferred_element_type=jnp.float32
                )
                s_ref[:, j * 256 : (j + 1) * 256] = s
                gate = jnp.where(t_ok & w_ok, 1.0, 0.0)
                ok = jnp.broadcast_to(marks[j : j + 1, 0:1] * gate, (256, 1)) > 0.5
                tops.append(jnp.where(ok, jnp.max(s, axis=1, keepdims=True), -BIG))
                oks.append(ok)
        peak = tops[0]
        for x in tops[1:]:
            peak = jnp.maximum(peak, x)
        peak = peak * SCALE
        total = jnp.zeros((256, 128), jnp.float32)
        acc = jnp.zeros((256, D), jnp.float32)
        for a, ref in enumerate((prev_ref, own_ref, next_ref)):
            for b in range(3):
                index = jnp.clip(w + b - 1 + half, 0, HALO - 1) + HALO
                j = 3 * a + b
                v = ref[:, index].reshape(256, D)
                shift = jnp.where(oks[j], peak, BIG)
                p = jnp.exp2(s_ref[:, j * 256 : (j + 1) * 256] * SCALE - shift)
                total = total + p[:, 0:128] + p[:, 128:256]
                acc = acc + jnp.dot(
                    p.astype(jnp.bfloat16), v, preferred_element_type=jnp.float32
                )
        out = acc / jnp.sum(total, axis=1, keepdims=True)
        o_ref[:, w] = out.astype(jnp.bfloat16).reshape(16, 16, D)
        return carry

    lax.fori_loop(0, TILES, tile, 0)


def attend(q, prev, own, nxt):
    vmem = pl.BlockSpec(memory_space=pltpu.VMEM)
    return pl.pallas_call(
        attend_kernel,
        out_shape=jax.ShapeDtypeStruct((16, TILES, 16, D), jnp.bfloat16),
        in_specs=[vmem] * 4,
        out_specs=vmem,
        scratch_shapes=[pltpu.VMEM((256, 9 * 256), jnp.float32)],
        name="attend",
    )(q, prev, own, nxt)


def unpack_kernel(x_ref, o_ref):
    for h in range(HEADS):
        for half in range(2):
            for r in range(2):
                o_ref[r, pl.ds(8 * half, TILES), :, pl.ds(h * D, D)] = x_ref[2 * h + half, :, r]


def unpack(x):
    vmem = pl.BlockSpec(memory_space=pltpu.VMEM)
    out = pl.pallas_call(
        unpack_kernel,
        out_shape=jax.ShapeDtypeStruct((2, COLS, 8, HEADS * D), jnp.bfloat16),
        in_specs=[vmem],
        out_specs=vmem,
        name="unpack",
    )(x)
    return out.reshape(256, HEADS * D)


def swap(x):
    return lax.all_to_all(x, "spatial", split_axis=0, concat_axis=0, tiled=True)


def body(queries, keys, values, window):
    kv_send, q_send = pack(queries, keys, values, window)
    own = swap(kv_send.reshape(16, 2 * HALO, 16, D))
    steps = lax.axis_size("temporal")
    up = [(i, i + 1) for i in range(steps - 1)]
    down = [(j, i) for i, j in up]
    prev = lax.ppermute(own, "temporal", up)
    nxt = lax.ppermute(own, "temporal", down)
    q = swap(q_send.reshape(16, TILES + 1, 16, D))
    out = attend(q, prev, own, nxt)
    back = swap(out)
    return unpack(back.reshape(16, TILES, 2, 8, D))


def solution(mesh):
    return jax.shard_map(
        body,
        mesh=mesh,
        in_specs=(
            P(("temporal", "spatial"), "head"),
            P(("temporal", "spatial"), "head"),
            P(("temporal", "spatial"), "head"),
            P("temporal", None, "spatial", None),
        ),
        out_specs=P(("temporal", "spatial"), "head"),
        check_vma=False,
    )
```

time: 208 us -> 84.7 us (0.41)
  waiting for transfers between devices: 91.2 us -> 0.01 us
  local copies, waits for them, and re-layouts: 34.7 us -> 3.2 us
  blocking collectives: 33.2 us -> 58.7 us
  starting transfers between devices: 23 us -> 4.32 us
  Pallas kernels: 0 us -> 17.8 us
  matrix products: 13.9 us -> 0 us
  other arithmetic: 10.1 us -> 0 us
    all_to_all x2 -> x0, waiting for transfers between devices: 78.9 us -> none  [the longest x1 68.5 us: body(): lax.all_to_all(to_blocks(queries), 'spatial', split_axis=0, concat_axis=0...]
    all_to_all x2 -> x3, blocking collectives: 33.2 us -> 58.7 us  [swap(): return lax.all_to_all(x, 'spatial', split_axis=0, concat_axis=0, tiled=True)]
    pallas_call x0 -> x3, Pallas kernels: none -> 17.8 us  [the longest x1 12.9 us: attend(): pl.pallas_call(attend_kernel, out_shape=jax.ShapeDtypeStruct((16, TILES,...]
    slice x6 -> x0, local copies, waits for them, and re-layouts: 17.4 us -> none  [the longest x2 5.43 us: body(): padded[1, :, :, row_low:row_high, 0:3].reshape(-1, heads_here, D_HEAD)]
    dot_general x8 -> x0, matrix products: 13.9 us -> none  [the longest x4 8.17 us: attend(): jnp.einsum('qhd,khd->hqk', query_part, key_part, preferred_element_type=j...]
    all_to_all x2 -> x0, starting transfers between devices: 13.3 us -> none  [the longest x1 7.03 us: body(): lax.all_to_all(to_blocks(keys), 'spatial', split_axis=0, concat_axis=0, t...]
    ppermute x4 -> x2, waiting for transfers between devices: 12.3 us -> 0.01 us  [the longest x1 0.01 us: body(): nxt = lax.ppermute(own, 'temporal', down)]
    concatenate x3 -> x0, other arithmetic: 6.74 us -> none  [the longest x2 6.68 us: with_halo(): array = jnp.concatenate([before, array, after], axis=dim)]
  transfers between devices with their start and end apart: 6 -> 2, of which waited for: 4 -> 0; matrix products, arithmetic and copies ran while one was open for 3% -> 0% of each run, Pallas kernels for 0% -> 0%
where the time goes in v1:
time: 84.7 us; the launch traced here: 84.1 us
  blocking collectives  58.7 us (69%)
  Pallas kernels  17.8 us (21%)
  starting transfers between devices  4.32 us (5%)
  local copies, waits for them, and re-layouts  3.2 us (4%)
    all_to_all x3, blocking collectives, swap(): return lax.all_to_all(x, 'spatial', split_axis=0, concat_axis=0, tiled=True)  58.7 us
    pallas_call x1, Pallas kernels, attend(): pl.pallas_call(attend_kernel, out_shape=jax.ShapeDtypeStruct((16, TILES,...  12.9 us
    pallas_call x1, Pallas kernels, pack(): pl.pallas_call(pack_kernel, out_shape=(jax.ShapeDtypeStruct((16, 2 * HALO...  2.9 us
    ppermute x1, starting transfers between devices, body(): prev = lax.ppermute(own, 'temporal', up)  2.41 us
    unnamed x8, local copies, waits for them, and re-layouts  2.03 us
    pallas_call x1, Pallas kernels, unpack(): pl.pallas_call(unpack_kernel, out_shape=jax.ShapeDtypeStruct((2, COLS, 8,...  1.98 us
    ppermute x1, starting transfers between devices, body(): nxt = lax.ppermute(own, 'temporal', down)  1.91 us
  transfers between devices with their start and end apart: 2, of which 0 were waited for; matrix products, arithmetic and copies ran while one was open for 0% of the time, Pallas kernels for 0%

profile of v1, /device:TPU:32, one launch (start us, length us, event | category | flops | bytes accessed | tf_op | source)
XLA Modules:
  0.0 84.1 jit_solution(6554450445088083550)
XLA Ops:
  0.0 1.2 %pad.4.w_ref = s32[1,128]{1,0:T(1,128)} pad(s32[1,27]{1,0:T(1,128)} %bitcast.14, s32[]{:T(128)} %constant.0.clone.1), padding=0_0x0_101 | pad | bytes 624 | tf_op jit(solution)/shard_map/jit(_pad)/pad | solution.py:42
  1.2 2.9 %pack.1 = (bf16[16,18,2,8,128]{4,3,2,1,0:T(8,128)(2,1)}, bf16[16,9,2,8,128]{4,3,2,1,0:T(8,128)(2,1)}) custom-call(bf16[2,16,8,1024]{3,2,1,0:T(8,128)(2,1)} %bitcast.11, bf16[2,16,8,1024]{3,2,1,0:T(8,128)(2,1)} %bitcast.12, bf16[2,16,8,1024]{3,2,1,0:T(8,128)(2,1)} %bitcast.13, s32[1,128]{1,0:T(1,128)} %pad.4.w_ref), custom_call_target="tpu_custom_call" | custom-call | tf_op jit(solution)/shard_map/pack/pallas_call | solution.py:44
  4.1 0.0 copy-start.3
  4.1 25.7 %all_to_all.15.own_ref = bf16[16,18,16,128]{3,2,1,0:T(8,128)(2,1)S(1)} all-to-all(bf16[16,18,16,128]{3,2,1,0:T(8,128)(2,1)} %bitcast.9), channel_id=1, replica_groups=mesh['temporal'=8,'spatial'=16,'head'=2] {'spatial'}, dimensions={0} | all-to-all | bytes 2359296 | tf_op jit(solution)/shard_map/all_to_all | solution.py:136
  29.8 0.0 copy-start
  29.8 1.9 %collective-permute-start.1 = (bf16[16,18,16,128]{3,2,1,0:T(8,128)(2,1)S(1)}, bf16[16,18,16,128]{3,2,1,0:T(8,128)(2,1)S(1)}, u32[]{:S(2)}, u32[]{:S(2)}) collective-permute-start(bf16[16,18,16,128]{3,2,1,0:T(8,128)(2,1)S(1)} %all_to_all.15.own_ref), channel_id=1, source_target_pairs={{32,0},{64,32},{96,64},{128,96},{160,128},{192,160},{224,192},{33,... | collective-permute-start | bytes 3538952 | tf_op jit(solution)/shard_map/ppermute | solution.py:146
  31.7 2.4 %collective-permute-start = (bf16[16,18,16,128]{3,2,1,0:T(8,128)(2,1)S(1)}, bf16[16,18,16,128]{3,2,1,0:T(8,128)(2,1)S(1)}, u32[]{:S(2)}, u32[]{:S(2)}) collective-permute-start(bf16[16,18,16,128]{3,2,1,0:T(8,128)(2,1)S(1)} %all_to_all.15.own_ref), channel_id=1, source_target_pairs={{0,32},{32,64},{64,96},{96,128},{128,160},{160,192},{192,224},{1,3... | collective-permute-start | bytes 3538952 | tf_op jit(solution)/shard_map/ppermute | solution.py:145
  34.1 0.0 copy-done.3
  34.1 16.4 %all_to_all.16.q_ref = bf16[16,9,16,128]{3,2,1,0:T(8,128)(2,1)} all-to-all(bf16[16,9,16,128]{3,2,1,0:T(8,128)(2,1)S(1)} %bitcast.10), channel_id=1, replica_groups=mesh['temporal'=8,'spatial'=16,'head'=2] {'spatial'}, dimensions={0} | all-to-all | bytes 1179648 | tf_op jit(solution)/shard_map/all_to_all | solution.py:136
  50.5 0.0 collective-permute-done.1.next_ref
  50.5 0.0 copy-start.1
  50.5 0.0 collective-permute-done.prev_ref
  50.5 0.0 copy-done
  50.5 1.0 %copy-done.1 = bf16[16,18,16,128]{3,2,1,0:T(8,128)(2,1)} copy-done((bf16[16,18,16,128]{3,2,1,0:T(8,128)(2,1)}, bf16[16,18,16,128]{3,2,1,0:T(8,128)(2,1)S(1)}, u32[]{:S(2)}) %copy-start.1) | copy-done | bytes 1179672
  51.5 0.0 copy-start.2
  51.5 1.0 %copy-done.2 = bf16[16,18,16,128]{3,2,1,0:T(8,128)(2,1)} copy-done((bf16[16,18,16,128]{3,2,1,0:T(8,128)(2,1)}, bf16[16,18,16,128]{3,2,1,0:T(8,128)(2,1)S(1)}, u32[]{:S(2)}) %copy-start.2) | copy-done | bytes 1179672
  52.5 12.9 %attend.1 = bf16[16,8,16,128]{3,2,1,0:T(8,128)(2,1)} custom-call(bf16[16,9,16,128]{3,2,1,0:T(8,128)(2,1)} %all_to_all.16.q_ref, bf16[16,18,16,128]{3,2,1,0:T(8,128)(2,1)} %copy-done.2, bf16[16,18,16,128]{3,2,1,0:T(8,128)(2,1)} %copy-done, bf16[16,18,16,128]{3,2,1,0:T(8,128)(2,1)} %copy-done.1), custom_call_target="tpu_custom_call" | custom-call | tf_op jit(solution)/shard_map/attend/pallas_call | solution.py:106
  65.5 16.6 %all_to_all.17 = bf16[16,8,16,128]{3,2,1,0:T(8,128)(2,1)} all-to-all(bf16[16,8,16,128]{3,2,1,0:T(8,128)(2,1)} %attend.1), channel_id=1, replica_groups=mesh['temporal'=8,'spatial'=16,'head'=2] {'spatial'}, dimensions={0} | all-to-all | bytes 1048576 | tf_op jit(solution)/shard_map/all_to_all | solution.py:136
  82.1 2.0 %unpack.1 = bf16[2,16,8,1024]{3,2,1,0:T(8,128)(2,1)} custom-call(bf16[16,8,2,8,128]{4,3,2,1,0:T(8,128)(2,1)} %bitcast.8), custom_call_target="tpu_custom_call" | custom-call | tf_op jit(solution)/shard_map/unpack/pallas_call | solution.py:125
Async XLA Ops:
  4.1 30.1 %copy-start.3 = (bf16[16,9,2,8,128]{4,3,2,1,0:T(8,128)(2,1)S(1)}, bf16[16,9,2,8,128]{4,3,2,1,0:T(8,128)(2,1)}, u32[]{:S(2)}) copy-start(bf16[16,9,2,8,128]{4,3,2,1,0:T(8,128)(2,1)} %get-tuple-element.7) | copy-start | bytes 1769476
  29.8 20.7 %copy-start = (bf16[16,18,16,128]{3,2,1,0:T(8,128)(2,1)}, bf16[16,18,16,128]{3,2,1,0:T(8,128)(2,1)S(1)}, u32[]{:S(2)}) copy-start(bf16[16,18,16,128]{3,2,1,0:T(8,128)(2,1)S(1)} %all_to_all.15.own_ref) | copy-start | bytes 3538948
  29.8 20.7 %collective-permute-start.1 = (bf16[16,18,16,128]{3,2,1,0:T(8,128)(2,1)S(1)}, bf16[16,18,16,128]{3,2,1,0:T(8,128)(2,1)S(1)}, u32[]{:S(2)}, u32[]{:S(2)}) collective-permute-start(bf16[16,18,16,128]{3,2,1,0:T(8,128)(2,1)S(1)} %all_to_all.15.own_ref), channel_id=1, source_target_pairs={{32,0},{64,32},{96,64},{128,96},{160,128},{192,160},{224,192},{33,... | collective-permute-start | bytes 3538952 | tf_op jit(solution)/shard_map/ppermute | solution.py:146
  31.7 18.8 %collective-permute-start = (bf16[16,18,16,128]{3,2,1,0:T(8,128)(2,1)S(1)}, bf16[16,18,16,128]{3,2,1,0:T(8,128)(2,1)S(1)}, u32[]{:S(2)}, u32[]{:S(2)}) collective-permute-start(bf16[16,18,16,128]{3,2,1,0:T(8,128)(2,1)S(1)} %all_to_all.15.own_ref), channel_id=1, source_target_pairs={{0,32},{32,64},{64,96},{96,128},{128,160},{160,192},{192,224},{1,3... | collective-permute-start | bytes 3538952 | tf_op jit(solution)/shard_map/ppermute | solution.py:145
  50.5 1.0 %copy-start.1 = (bf16[16,18,16,128]{3,2,1,0:T(8,128)(2,1)}, bf16[16,18,16,128]{3,2,1,0:T(8,128)(2,1)S(1)}, u32[]{:S(2)}) copy-start(bf16[16,18,16,128]{3,2,1,0:T(8,128)(2,1)S(1)} %collective-permute-done.1.next_ref) | copy-start | bytes 3538948
  51.5 1.0 %copy-start.2 = (bf16[16,18,16,128]{3,2,1,0:T(8,128)(2,1)}, bf16[16,18,16,128]{3,2,1,0:T(8,128)(2,1)S(1)}, u32[]{:S(2)}) copy-start(bf16[16,18,16,128]{3,2,1,0:T(8,128)(2,1)S(1)} %collective-permute-done.prev_ref) | copy-start | bytes 3538948

commit v2 on v1

--- a/solution.py
+++ b/solution.py
@@ -16,8 +16,13 @@
 SCALE = math.log2(math.e) / math.sqrt(D)
 
 
+def resident(x):
+    return pltpu.with_memory_space_constraint(x, pltpu.VMEM)
+
+
 def pack_kernel(q_ref, k_ref, v_ref, w_ref, kv_out, q_out):
     pattern = w_ref[...].astype(jnp.float32)
+    pattern = jnp.concatenate([pattern, jnp.zeros((1, 101), jnp.float32)], axis=1)
     rows = lax.broadcasted_iota(jnp.int32, (16, 128), 0)
     lanes = lax.broadcasted_iota(jnp.int32, (16, 128), 1)
     pick = 9 * (rows // 3) + 3 + rows % 3
@@ -39,17 +44,18 @@
 
 def pack(q, k, v, window):
     shaped = [x.reshape(2, COLS, 8, HEADS * D) for x in (q, k, v)]
-    pattern = jnp.pad(window.reshape(1, 27), ((0, 0), (0, 101)))
+    pattern = window.reshape(1, 27)
     vmem = pl.BlockSpec(memory_space=pltpu.VMEM)
     return pl.pallas_call(
         pack_kernel,
         out_shape=(
-            jax.ShapeDtypeStruct((16, 2 * HALO, 2, 8, D), jnp.bfloat16),
-            jax.ShapeDtypeStruct((16, TILES + 1, 2, 8, D), jnp.bfloat16),
+            pltpu.VMEM((16, 2 * HALO, 2, 8, D), jnp.bfloat16),
+            pltpu.VMEM((16, TILES + 1, 2, 8, D), jnp.bfloat16),
         ),
         in_specs=[vmem] * 4,
         out_specs=(vmem, vmem),
         name="pack",
+        compiler_params=pltpu.CompilerParams(vmem_limit_bytes=16 << 20),
     )(*shaped, pattern)
 
 
@@ -105,12 +111,13 @@
     vmem = pl.BlockSpec(memory_space=pltpu.VMEM)
     return pl.pallas_call(
         attend_kernel,
-        out_shape=jax.ShapeDtypeStruct((16, TILES, 16, D), jnp.bfloat16),
+        out_shape=pltpu.VMEM((16, TILES, 16, D), jnp.bfloat16),
         in_specs=[vmem] * 4,
         out_specs=vmem,
         scratch_shapes=[pltpu.VMEM((256, 9 * 256), jnp.float32)],
         name="attend",
-    )(q, prev, own, nxt)
+        compiler_params=pltpu.CompilerParams(vmem_limit_bytes=24 << 20),
+    )(*[resident(x) for x in (q, prev, own, nxt)])
 
 
 def unpack_kernel(x_ref, o_ref):
@@ -128,7 +135,8 @@
         in_specs=[vmem],
         out_specs=vmem,
         name="unpack",
-    )(x)
+        compiler_params=pltpu.CompilerParams(vmem_limit_bytes=8 << 20),
+    )(resident(x))
     return out.reshape(256, HEADS * D)
 
 

time: 84.7 us -> 76.6 us (0.904)
  Pallas kernels: 17.8 us -> 11.2 us
  blocking collectives: 58.7 us -> 56.8 us
    pallas_call x2, Pallas kernels: 15.8 us -> 10.3 us  [the longest x1 10 us: attend(): pl.pallas_call(attend_kernel, out_shape=pltpu.VMEM((16, TILES, 16, D), jn...]
    all_to_all x3, blocking collectives: 58.7 us -> 56.8 us  [swap(): return lax.all_to_all(x, 'spatial', split_axis=0, concat_axis=0, tiled=True)]
    unnamed x8, local copies, waits for them, and re-layouts: 2.03 us -> 3.78 us
    pad x1 -> x0, local copies, waits for them, and re-layouts: 1.17 us -> none  [pack(): pattern = jnp.pad(window.reshape(1, 27), ((0, 0), (0, 101)))]
    pallas_call x1, Pallas kernels: 1.98 us -> 0.94 us  [unpack(): pl.pallas_call(unpack_kernel, out_shape=jax.ShapeDtypeStruct((2, COLS, 8,...]
where the time goes in v2:
time: 76.6 us; the launch traced here: 76.2 us
  blocking collectives  56.8 us (74%)
  Pallas kernels  11.2 us (15%)
  starting transfers between devices  4.32 us (6%)
  local copies, waits for them, and re-layouts  3.78 us (5%)
    all_to_all x3, blocking collectives, swap(): return lax.all_to_all(x, 'spatial', split_axis=0, concat_axis=0, tiled=True)  56.8 us
    pallas_call x1, Pallas kernels, attend(): pl.pallas_call(attend_kernel, out_shape=pltpu.VMEM((16, TILES, 16, D), jn...  10 us
    unnamed x8, local copies, waits for them, and re-layouts  3.78 us
    ppermute x1, starting transfers between devices, body(): prev = lax.ppermute(own, 'temporal', up)  2.41 us
    ppermute x1, starting transfers between devices, body(): nxt = lax.ppermute(own, 'temporal', down)  1.91 us
  transfers between devices with their start and end apart: 2, of which 0 were waited for; matrix products, arithmetic and copies ran while one was open for 0% of the time, Pallas kernels for 0%

profile of v2, /device:TPU:32, one launch (start us, length us, event | category | flops | bytes accessed | tf_op | source)
XLA Modules:
  0.0 76.2 jit_solution(7629026406630789649)
XLA Ops:
  0.0 0.0 copy-start
  0.0 1.0 %copy-done = bf16[256,1024]{1,0:T(8,128)(2,1)S(1)} copy-done((bf16[256,1024]{1,0:T(8,128)(2,1)S(1)}, bf16[256,1024]{1,0:T(8,128)(2,1)}, u32[]{:S(2)}) %copy-start) | copy-done | bytes 524312
  1.0 0.0 copy-start.1
  1.0 1.0 %copy-done.1 = bf16[256,1024]{1,0:T(8,128)(2,1)S(1)} copy-done((bf16[256,1024]{1,0:T(8,128)(2,1)S(1)}, bf16[256,1024]{1,0:T(8,128)(2,1)}, u32[]{:S(2)}) %copy-start.1) | copy-done | bytes 524312
  2.1 0.0 copy-start.2
  2.1 1.0 %copy-done.2 = bf16[256,1024]{1,0:T(8,128)(2,1)S(1)} copy-done((bf16[256,1024]{1,0:T(8,128)(2,1)S(1)}, bf16[256,1024]{1,0:T(8,128)(2,1)}, u32[]{:S(2)}) %copy-start.2) | copy-done | bytes 524312
  3.1 0.0 copy-start.3
  3.1 0.7 copy-done.3
  3.8 0.3 pack.1
  4.1 25.4 %all_to_all.15.own_ref = bf16[16,18,16,128]{3,2,1,0:T(8,128)(2,1)S(1)} all-to-all(bf16[16,18,16,128]{3,2,1,0:T(8,128)(2,1)S(1)} %bitcast.9), channel_id=1, replica_groups=mesh['temporal'=8,'spatial'=16,'head'=2] {'spatial'}, dimensions={0} | all-to-all | bytes 2359296 | tf_op jit(solution)/shard_map/all_to_all | solution.py:144
  29.5 1.9 %collective-permute-start.1 = (bf16[16,18,16,128]{3,2,1,0:T(8,128)(2,1)S(1)}, bf16[16,18,16,128]{3,2,1,0:T(8,128)(2,1)S(1)}, u32[]{:S(2)}, u32[]{:S(2)}) collective-permute-start(bf16[16,18,16,128]{3,2,1,0:T(8,128)(2,1)S(1)} %all_to_all.15.own_ref), channel_id=1, source_target_pairs={{32,0},{64,32},{96,64},{128,96},{160,128},{192,160},{224,192},{33,... | collective-permute-start | bytes 3538952 | tf_op jit(solution)/shard_map/ppermute | solution.py:154
  31.4 2.4 %collective-permute-start = (bf16[16,18,16,128]{3,2,1,0:T(8,128)(2,1)S(1)}, bf16[16,18,16,128]{3,2,1,0:T(8,128)(2,1)S(1)}, u32[]{:S(2)}, u32[]{:S(2)}) collective-permute-start(bf16[16,18,16,128]{3,2,1,0:T(8,128)(2,1)S(1)} %all_to_all.15.own_ref), channel_id=1, source_target_pairs={{0,32},{32,64},{64,96},{96,128},{128,160},{160,192},{192,224},{1,3... | collective-permute-start | bytes 3538952 | tf_op jit(solution)/shard_map/ppermute | solution.py:153
  33.8 16.4 %all_to_all.16.q_ref = bf16[16,9,16,128]{3,2,1,0:T(8,128)(2,1)S(1)} all-to-all(bf16[16,9,16,128]{3,2,1,0:T(8,128)(2,1)S(1)} %bitcast.10), channel_id=1, replica_groups=mesh['temporal'=8,'spatial'=16,'head'=2] {'spatial'}, dimensions={0} | all-to-all | bytes 1179648 | tf_op jit(solution)/shard_map/all_to_all | solution.py:144
  50.3 0.0 collective-permute-done.1.next_ref
  50.3 0.0 collective-permute-done.prev_ref
  50.3 10.0 %attend.1 = bf16[16,8,16,128]{3,2,1,0:T(8,128)(2,1)S(1)} custom-call(bf16[16,9,16,128]{3,2,1,0:T(8,128)(2,1)S(1)} %all_to_all.16.q_ref, bf16[16,18,16,128]{3,2,1,0:T(8,128)(2,1)S(1)} %collective-permute-done.prev_ref, bf16[16,18,16,128]{3,2,1,0:T(8,128)(2,1)S(1)} %all_to_all.15.own_ref, bf16[16,18,16,128]{3,2,1,0:T(8,128)(2,1)S(1)} %collective-permute-done.1.next_ref), custom_call_target="tpu_custom_call" | custom-call | tf_op jit(solution)/shard_map/attend/pallas_call | solution.py:112
  60.3 15.0 %all_to_all.17 = bf16[16,8,16,128]{3,2,1,0:T(8,128)(2,1)S(1)} all-to-all(bf16[16,8,16,128]{3,2,1,0:T(8,128)(2,1)S(1)} %attend.1), channel_id=1, replica_groups=mesh['temporal'=8,'spatial'=16,'head'=2] {'spatial'}, dimensions={0} | all-to-all | bytes 1048576 | tf_op jit(solution)/shard_map/all_to_all | solution.py:144
  75.2 0.9 %unpack.1 = bf16[2,16,8,1024]{3,2,1,0:T(8,128)(2,1)} custom-call(bf16[16,8,2,8,128]{4,3,2,1,0:T(8,128)(2,1)S(1)} %bitcast.8), custom_call_target="tpu_custom_call" | custom-call | tf_op jit(solution)/shard_map/unpack/pallas_call | solution.py:132
Async XLA Ops:
  0.0 1.0 %copy-start = (bf16[256,1024]{1,0:T(8,128)(2,1)S(1)}, bf16[256,1024]{1,0:T(8,128)(2,1)}, u32[]{:S(2)}) copy-start(bf16[256,1024]{1,0:T(8,128)(2,1)} %param.4) | copy-start | bytes 1572868
  1.0 1.0 %copy-start.1 = (bf16[256,1024]{1,0:T(8,128)(2,1)S(1)}, bf16[256,1024]{1,0:T(8,128)(2,1)}, u32[]{:S(2)}) copy-start(bf16[256,1024]{1,0:T(8,128)(2,1)} %param.5) | copy-start | bytes 1572868
  2.1 1.0 %copy-start.2 = (bf16[256,1024]{1,0:T(8,128)(2,1)S(1)}, bf16[256,1024]{1,0:T(8,128)(2,1)}, u32[]{:S(2)}) copy-start(bf16[256,1024]{1,0:T(8,128)(2,1)} %param.6) | copy-start | bytes 1572868
  3.1 0.7 copy-start.3
  29.5 20.8 %collective-permute-start.1 = (bf16[16,18,16,128]{3,2,1,0:T(8,128)(2,1)S(1)}, bf16[16,18,16,128]{3,2,1,0:T(8,128)(2,1)S(1)}, u32[]{:S(2)}, u32[]{:S(2)}) collective-permute-start(bf16[16,18,16,128]{3,2,1,0:T(8,128)(2,1)S(1)} %all_to_all.15.own_ref), channel_id=1, source_target_pairs={{32,0},{64,32},{96,64},{128,96},{160,128},{192,160},{224,192},{33,... | collective-permute-start | bytes 3538952 | tf_op jit(solution)/shard_map/ppermute | solution.py:154
  31.4 18.9 %collective-permute-start = (bf16[16,18,16,128]{3,2,1,0:T(8,128)(2,1)S(1)}, bf16[16,18,16,128]{3,2,1,0:T(8,128)(2,1)S(1)}, u32[]{:S(2)}, u32[]{:S(2)}) collective-permute-start(bf16[16,18,16,128]{3,2,1,0:T(8,128)(2,1)S(1)} %all_to_all.15.own_ref), channel_id=1, source_target_pairs={{0,32},{32,64},{64,96},{96,128},{128,160},{160,192},{192,224},{1,3... | collective-permute-start | bytes 3538952 | tf_op jit(solution)/shard_map/ppermute | solution.py:153

commit v3 on v2

v3 whole, which is shorter than its diff:
```python
import math

import jax
import jax.numpy as jnp
from jax import lax
from jax.experimental import pallas as pl
from jax.experimental.pallas import tpu as pltpu
from jax.sharding import PartitionSpec as P

D = 128
HEADS = 8
TILES = 8
COLS = 16
HALO = 9
KV_ROWS = 2 * HALO * 16
Q_ROW = KV_ROWS
MARK_ROW = KV_ROWS + TILES * 16
ROWS = MARK_ROW + 8
BIG = 3.0e38
SCALE = math.log2(math.e) / math.sqrt(D)
VMEM = pl.BlockSpec(memory_space=pltpu.VMEM)


def resident(x):
    return pltpu.with_memory_space_constraint(x, pltpu.VMEM)


def limit(mib):
    return pltpu.CompilerParams(vmem_limit_bytes=mib << 20)


def pack_kernel(q_hbm, k_hbm, v_hbm, w_ref, out, buf, sems):
    copies = []
    for i, src in enumerate((k_hbm, v_hbm, q_hbm)):
        for r in range(2):
            for part in range(2):
                cut = pl.ds(8 * part, 8)
                copies.append(
                    pltpu.make_async_copy(
                        src.at[r, cut], buf.at[i, r, cut], sems.at[i, r, part]
                    )
                )
    for copy in copies:
        copy.start()
    pattern = w_ref[...].astype(jnp.float32)
    pattern = jnp.concatenate([pattern, jnp.zeros((1, 101), jnp.float32)], axis=1)
    row = lax.broadcasted_iota(jnp.int32, (8, 128), 0)
    lanes = lax.broadcasted_iota(jnp.int32, (8, 128), 1)
    entry = row + jnp.where(row >= 4, 1, 0)
    pick = 9 * (entry // 3) + 3 + entry % 3
    kept = jnp.where(lanes == pick, jnp.broadcast_to(pattern, (8, 128)), 0.0)
    marks = jnp.broadcast_to(jnp.sum(kept, axis=1, keepdims=True), (8, 128))
    marks = marks.astype(jnp.bfloat16)
    for d in range(16):
        out[d, MARK_ROW // 8] = marks
    for i in range(3):
        for copy in copies[4 * i : 4 * i + 4]:
            copy.wait()
        count, step = (TILES, 8) if i == 2 else (HALO, 7)
        base = (0, 2 * HALO, Q_ROW // 8)[i]
        for h in range(HEADS):
            for half in range(2):
                for r in range(2):
                    for w in range(count):
                        out[2 * h + half, base + 2 * w + r] = buf[
                            i, r, step * half + w, :, pl.ds(h * D, D)
                        ]


def pack(q, k, v, window):
    shaped = [
        pltpu.with_memory_space_constraint(x.reshape(2, COLS, 8, HEADS * D), pltpu.HBM)
        for x in (q, k, v)
    ]
    anywhere = pl.BlockSpec(memory_space=pl.ANY)
    return pl.pallas_call(
        pack_kernel,
        out_shape=pltpu.VMEM((16, ROWS // 8, 8, D), jnp.bfloat16),
        in_specs=[anywhere] * 3 + [VMEM],
        out_specs=VMEM,
        scratch_shapes=[
            pltpu.VMEM((3, 2, COLS, 8, HEADS * D), jnp.bfloat16),
            pltpu.SemaphoreType.DMA((3, 2, 2)),
        ],
        compiler_params=limit(16),
        name="pack",
    )(*shaped, window.reshape(1, 27))


def cut_kernel(all_ref, kv_ref):
    kv_ref[...] = all_ref[:, 0:KV_ROWS]


def cut(everything):
    return pl.pallas_call(
        cut_kernel,
        out_shape=pltpu.VMEM((16, KV_ROWS, D), jnp.bfloat16),
        in_specs=[VMEM],
        out_specs=VMEM,
        compiler_params=limit(8),
        name="cut",
    )(resident(everything))


def take(ref, row):
    start = pl.multiple_of(row, 16)
    return ref[:, pl.ds(start, 16), :].reshape(256, D)


def shard_place():
    t = lax.axis_index("temporal")
    half = lax.axis_index("spatial") % 2
    return t, half


def key_index(w, b, half):
    return jnp.clip(w + b - 1 + half, 0, HALO - 1)


def columns_ok(column, b):
    return (column + b - 1 >= 0) & (column + b - 1 < COLS)


def scores(q, k):
    return lax.dot_general(q, k, (((1,), (1,)), ((), ())), preferred_element_type=jnp.float32)


def weigh(s_ref, slot, refs, oks, shift_from, w, half, total, acc):
    for n, (ref, b) in enumerate(refs):
        v = take(ref, (key_index(w, b, half) + HALO) * 16)
        shift = shift_from if oks[n] is None else jnp.where(oks[n], shift_from, BIG)
        p = jnp.exp2(s_ref[slot, :, n * 256 : (n + 1) * 256] * SCALE - shift)
        part = p[:, 0:128] + p[:, 128:256]
        total = part if total is None else total + part
        mixed = jnp.dot(p.astype(jnp.bfloat16), v, preferred_element_type=jnp.float32)
        acc = mixed if acc is None else acc + mixed
    return total, acc


def near_kernel(all_ref, mate_ref, acc_ref, peak_ref, total_ref, s_ref):
    t, half = shard_place()
    even = t % 2 == 0

    def tile(w, slot):
        column = half * TILES + w
        q = take(all_ref, Q_ROW + 16 * w)
        marks = all_ref[column, pl.ds(MARK_ROW, 8), :].astype(jnp.float32)
        refs, oks, top = [], [], None
        for ref in (all_ref, mate_ref):
            for b in range(3):
                n = len(refs)
                k = take(ref, key_index(w, b, half) * 16)
                s = scores(q, k)
                s_ref[slot, :, n * 256 : (n + 1) * 256] = s
                high = jnp.max(s, axis=1, keepdims=True)
                if ref is all_ref:
                    mark = None if b == 1 else marks[3 + b // 2 : 4 + b // 2, 0:1]
                else:
                    mark = jnp.where(even, marks[5 + b : 6 + b, 0:1], marks[b : b + 1, 0:1])
                if mark is None:
                    ok = None
                else:
                    gate = 1.0 if b == 1 else jnp.where(columns_ok(column, b), 1.0, 0.0)
                    ok = jnp.broadcast_to(mark * gate, (256, 1)) > 0.5
                    high = jnp.where(ok, high, -BIG)
                top = high if top is None else jnp.maximum(top, high)
                refs.append((ref, b))
                oks.append(ok)
        peak = top * SCALE
        total, acc = weigh(s_ref, slot, refs, oks, peak, w, half, None, None)
        acc_ref[w] = acc
        total_ref[w] = total
        peak_ref[w] = jnp.broadcast_to(peak, (256, 128))

    def pair(i, carry):
        tile(2 * i, 0)
        tile(2 * i + 1, 1)
        return carry

    lax.fori_loop(0, TILES // 2, pair, 0)


def near(everything, mate):
    part = pltpu.VMEM((TILES, 256, D), jnp.float32)
    return pl.pallas_call(
        near_kernel,
        out_shape=(part, part, part),
        in_specs=[VMEM] * 2,
        out_specs=(VMEM,) * 3,
        scratch_shapes=[pltpu.VMEM((2, 256, 6 * 256), jnp.float32)],
        compiler_params=limit(16),
        cost_estimate=pl.CostEstimate(
            flops=8 * 6 * 4 * 256 * 256 * D, bytes_accessed=6 << 20, transcendentals=8 * 6 * 65536
        ),
        name="near",
    )(resident(everything), resident(mate))


def far_kernel(all_ref, far_ref, acc_ref, peak_ref, total_ref, o_ref, s_ref):
    t, half = shard_place()
    even = t % 2 == 0
    t_ok = jnp.where(even, t > 0, t < 7)

    def tile(w, slot):
        column = half * TILES + w
        q = take(all_ref, Q_ROW + 16 * w)
        marks = all_ref[column, pl.ds(MARK_ROW, 8), :].astype(jnp.float32)
        refs, oks = [], []
        before = peak_ref[w, :, 0:1]
        top = None
        for b in range(3):
            k = take(far_ref, key_index(w, b, half) * 16)
            s = scores(q, k)
            s_ref[slot, :, b * 256 : (b + 1) * 256] = s
            mark = jnp.where(even, marks[b : b + 1, 0:1], marks[5 + b : 6 + b, 0:1])
            gate = jnp.where(columns_ok(column, b) & t_ok, 1.0, 0.0)
            ok = jnp.broadcast_to(mark * gate, (256, 1)) > 0.5
            high = jnp.where(ok, jnp.max(s, axis=1, keepdims=True), -BIG)
            top = high if top is None else jnp.maximum(top, high)
            refs.append((far_ref, b))
            oks.append(ok)
        peak = jnp.maximum(before, jnp.where(top > -BIG, top, -BIG / 4) * SCALE)
        fade = jnp.exp2(before - peak)
        total, acc = weigh(
            s_ref, slot, refs, oks, peak, w, half, total_ref[w] * fade, acc_ref[w] * fade
        )
        out = acc / jnp.sum(total, axis=1, keepdims=True)
        o_ref[:, pl.ds(pl.multiple_of(16 * w, 16), 16), :] = out.astype(jnp.bfloat16).reshape(
            16, 16, D
        )

    def pair(i, carry):
        tile(2 * i, 0)
        tile(2 * i + 1, 1)
        return carry

    lax.fori_loop(0, TILES // 2, pair, 0)


def far(everything, other, parts):
    return pl.pallas_call(
        far_kernel,
        out_shape=pltpu.VMEM((16, TILES * 16, D), jnp.bfloat16),
        in_specs=[VMEM] * 5,
        out_specs=VMEM,
        scratch_shapes=[pltpu.VMEM((2, 256, 3 * 256), jnp.float32)],
        compiler_params=limit(16),
        name="far",
    )(*[resident(x) for x in (everything, other, *parts)])


def unpack_kernel(x_ref, o_ref):
    for h in range(HEADS):
        for half in range(2):
            for r in range(2):
                o_ref[r, pl.ds(8 * half, TILES), :, pl.ds(h * D, D)] = x_ref[2 * h + half, :, r]


def unpack(x):
    out = pl.pallas_call(
        unpack_kernel,
        out_shape=jax.ShapeDtypeStruct((2, COLS, 8, HEADS * D), jnp.bfloat16),
        in_specs=[VMEM],
        out_specs=VMEM,
        compiler_params=limit(8),
        name="unpack",
    )(resident(x))
    return out.reshape(256, HEADS * D)


def swap(x):
    return lax.all_to_all(x, "spatial", split_axis=0, concat_axis=0, tiled=True)


def body(queries, keys, values, window):
    everything = swap(pack(queries, keys, values, window).reshape(16, ROWS, D))
    kv = cut(everything)
    steps = lax.axis_size("temporal")
    across = [(i, i + 1) for i in range(1, steps - 1, 2)]
    mates = [(i, i + 1) for i in range(0, steps, 2)]
    other = lax.ppermute(kv, "temporal", across + [(j, i) for i, j in across])
    mate = lax.ppermute(kv, "temporal", mates + [(j, i) for i, j in mates])
    parts = near(everything, mate)
    out = far(everything, other, parts)
    back = swap(out)
    return unpack(back.reshape(16, TILES, 2, 8, D))


def solution(mesh):
    return jax.shard_map(
        body,
        mesh=mesh,
        in_specs=(
            P(("temporal", "spatial"), "head"),
            P(("temporal", "spatial"), "head"),
            P(("temporal", "spatial"), "head"),
            P("temporal", None, "spatial", None),
        ),
        out_specs=P(("temporal", "spatial"), "head"),
        check_vma=False,
    )
```

time: 76.6 us -> 72.4 us (0.945)
  blocking collectives: 56.8 us -> 46.6 us
  waiting for transfers between devices: 0.01 us -> 8.82 us
  local copies, waits for them, and re-layouts: 3.78 us -> 0.65 us
  Pallas kernels: 11.2 us -> 13.9 us
  starting transfers between devices: 4.32 us -> 2.2 us
    all_to_all x3 -> x2, blocking collectives: 56.8 us -> 46.6 us  [swap(): return lax.all_to_all(x, 'spatial', split_axis=0, concat_axis=0, tiled=True)]
    ppermute x2, waiting for transfers between devices: 0.01 us -> 8.82 us  [the longest x1 8.1 us: body(): other = lax.ppermute(kv, 'temporal', across + [(j, i) for i, j in across])]
    unnamed x8 -> x2, local copies, waits for them, and re-layouts: 3.78 us -> 0.65 us
    pallas_call x2 -> x4, Pallas kernels: 10.3 us -> 12.9 us  [the longest x1 6.58 us: near(): pl.pallas_call(near_kernel, out_shape=(part, part, part), in_specs=[VMEM]...]
    ppermute x2, starting transfers between devices: 4.32 us -> 2.2 us  [the longest x1 2.11 us: body(): other = lax.ppermute(kv, 'temporal', across + [(j, i) for i, j in across])]
  transfers between devices with their start and end apart: 2 -> 2, of which waited for: 0 -> 2; matrix products, arithmetic and copies ran while one was open for 0% -> 0% of each run, Pallas kernels for 0% -> 9%
where the time goes in v3:
time: 72.4 us; the launch traced here: 72.2 us
  blocking collectives  46.6 us (64%)
  Pallas kernels  13.9 us (19%)
  waiting for transfers between devices  8.82 us (12%)
  starting transfers between devices  2.2 us (3%)
    all_to_all x2, blocking collectives, swap(): return lax.all_to_all(x, 'spatial', split_axis=0, concat_axis=0, tiled=True)  46.6 us
    ppermute x1, waiting for transfers between devices, body(): other = lax.ppermute(kv, 'temporal', across + [(j, i) for i, j in across])  8.1 us
    pallas_call x1, Pallas kernels, near(): pl.pallas_call(near_kernel, out_shape=(part, part, part), in_specs=[VMEM]...  6.58 us
    pallas_call x1, Pallas kernels, far(): pl.pallas_call(far_kernel, out_shape=pltpu.VMEM((16, TILES * 16, D), jnp....  4.64 us
    ppermute x1, starting transfers between devices, body(): other = lax.ppermute(kv, 'temporal', across + [(j, i) for i, j in across])  2.11 us
    pallas_call x1, Pallas kernels, pack(): pl.pallas_call(pack_kernel, out_shape=pltpu.VMEM((16, ROWS // 8, 8, D), j...  1.64 us
  transfers between devices with their start and end apart: 2, of which 2 were waited for; matrix products, arithmetic and copies ran while one was open for 0% of the time, Pallas kernels for 9%

profile of v3, /device:TPU:32, one launch (start us, length us, event | category | flops | bytes accessed | tf_op | source)
XLA Modules:
  0.0 72.2 jit_solution(15863160019102021815)
XLA Ops:
  0.0 0.0 copy-start
  0.0 0.7 copy-done
  0.7 1.6 %pack.1 = bf16[16,53,8,128]{3,2,1,0:T(8,128)(2,1)S(1)} custom-call(bf16[2,16,8,1024]{3,2,1,0:T(8,128)(2,1)} %bitcast.10, bf16[2,16,8,1024]{3,2,1,0:T(8,128)(2,1)} %bitcast.11, bf16[2,16,8,1024]{3,2,1,0:T(8,128)(2,1)} %bitcast.12, s32[1,27]{1,0:T(1,128)S(1)} %bitcast.9), custom_call_target="tpu_custom_call" | custom-call | tf_op jit(solution)/shard_map/pack/pallas_call | solution.py:76
  2.3 31.4 %all_to_all.10.all_ref = bf16[16,424,128]{2,1,0:T(8,128)(2,1)S(1)} all-to-all(bf16[16,424,128]{2,1,0:T(8,128)(2,1)S(1)} %bitcast.7), channel_id=1, replica_groups=mesh['temporal'=8,'spatial'=16,'head'=2] {'spatial'}, dimensions={0} | all-to-all | bytes 3473408 | tf_op jit(solution)/shard_map/all_to_all | solution.py:272
  33.7 0.1 cut.1
  33.7 0.1 collective-permute-start.1
  33.8 2.1 %collective-permute-start = (bf16[16,288,128]{2,1,0:T(8,128)(2,1)S(1)}, bf16[16,288,128]{2,1,0:T(8,128)(2,1)S(1)}, u32[]{:S(2)}, u32[]{:S(2)}) collective-permute-start(bf16[16,288,128]{2,1,0:T(8,128)(2,1)S(1)} %cut.1), channel_id=1, source_target_pairs={{32,64},{96,128},{160,192},{64,32},{128,96},{192,160},{33,65},{97,... | collective-permute-start | bytes 3538952 | tf_op jit(solution)/shard_map/ppermute | solution.py:281
  36.0 0.7 collective-permute-done.1.mate_ref
  36.7 6.6 %near.1 = (f32[8,256,128]{2,1,0:T(8,128)S(1)}, f32[8,256,128]{2,1,0:T(8,128)S(1)}, f32[8,256,128]{2,1,0:T(8,128)S(1)}) custom-call(bf16[16,424,128]{2,1,0:T(8,128)(2,1)S(1)} %all_to_all.10.all_ref, bf16[16,288,128]{2,1,0:T(8,128)(2,1)S(1)} %collective-permute-done.1.mate_ref), custom_call_target="tpu_custom_call" | custom-call | flops 1610612736 | bytes 6291456 | tf_op jit(solution)/shard_map/near/pallas_call | solution.py:185
  43.3 8.1 %collective-permute-done.far_ref = bf16[16,288,128]{2,1,0:T(8,128)(2,1)S(1)} collective-permute-done((bf16[16,288,128]{2,1,0:T(8,128)(2,1)S(1)}, bf16[16,288,128]{2,1,0:T(8,128)(2,1)S(1)}, u32[]{:S(2)}, u32[]{:S(2)}) %collective-permute-start) | collective-permute-done | bytes 1179680 | tf_op jit(solution)/shard_map/ppermute | solution.py:281
  51.4 4.6 %far.1 = bf16[16,128,128]{2,1,0:T(8,128)(2,1)S(1)} custom-call(bf16[16,424,128]{2,1,0:T(8,128)(2,1)S(1)} %all_to_all.10.all_ref, bf16[16,288,128]{2,1,0:T(8,128)(2,1)S(1)} %collective-permute-done.far_ref, f32[8,256,128]{2,1,0:T(8,128)S(1)} %get-tuple-element.8.acc_ref, f32[8,256,128]{2,1,0:T(8,128)S(1)} %get-tuple-element.9.peak_ref, ...), custom_call_target="tpu_custom_call" | custom-call | tf_op jit(solution)/shard_map/far/pallas_call | solution.py:241
  56.0 15.2 %all_to_all.11 = bf16[16,128,128]{2,1,0:T(8,128)(2,1)S(1)} all-to-all(bf16[16,128,128]{2,1,0:T(8,128)(2,1)S(1)} %far.1), channel_id=1, replica_groups=mesh['temporal'=8,'spatial'=16,'head'=2] {'spatial'}, dimensions={0} | all-to-all | bytes 1048576 | tf_op jit(solution)/shard_map/all_to_all | solution.py:272
  71.2 0.9 %unpack.1 = bf16[2,16,8,1024]{3,2,1,0:T(8,128)(2,1)} custom-call(bf16[16,8,2,8,128]{4,3,2,1,0:T(8,128)(2,1)S(1)} %bitcast.8), custom_call_target="tpu_custom_call" | custom-call | tf_op jit(solution)/shard_map/unpack/pallas_call | solution.py:260
Async XLA Ops:
  0.0 0.7 copy-start
  33.7 2.9 %collective-permute-start.1 = (bf16[16,288,128]{2,1,0:T(8,128)(2,1)S(1)}, bf16[16,288,128]{2,1,0:T(8,128)(2,1)S(1)}, u32[]{:S(2)}, u32[]{:S(2)}) collective-permute-start(bf16[16,288,128]{2,1,0:T(8,128)(2,1)S(1)} %cut.1), channel_id=1, source_target_pairs={{0,32},{64,96},{128,160},{192,224},{32,0},{96,64},{160,128},{224,1... | collective-permute-start | bytes 3538952 | tf_op jit(solution)/shard_map/ppermute | solution.py:282
  33.8 17.5 %collective-permute-start = (bf16[16,288,128]{2,1,0:T(8,128)(2,1)S(1)}, bf16[16,288,128]{2,1,0:T(8,128)(2,1)S(1)}, u32[]{:S(2)}, u32[]{:S(2)}) collective-permute-start(bf16[16,288,128]{2,1,0:T(8,128)(2,1)S(1)} %cut.1), channel_id=1, source_target_pairs={{32,64},{96,128},{160,192},{64,32},{128,96},{192,160},{33,65},{97,... | collective-permute-start | bytes 3538952 | tf_op jit(solution)/shard_map/ppermute | solution.py:281

commit v4 on v3

--- a/solution.py
+++ b/solution.py
@@ -1,3 +1,4 @@
+import functools
 import math
 
 import jax
@@ -16,6 +17,9 @@
 Q_ROW = KV_ROWS
 MARK_ROW = KV_ROWS + TILES * 16
 ROWS = MARK_ROW + 8
+FIRST = 7 * 16
+LAST = 2 * 16
+EARLY = 5
 BIG = 3.0e38
 SCALE = math.log2(math.e) / math.sqrt(D)
 VMEM = pl.BlockSpec(memory_space=pltpu.VMEM)
@@ -29,7 +33,9 @@
     return pltpu.CompilerParams(vmem_limit_bytes=mib << 20)
 
 
-def pack_kernel(q_hbm, k_hbm, v_hbm, w_ref, out, buf, sems):
+def pack_kernel(q_hbm, k_hbm, v_hbm, w_hbm, out, buf, w_ref, sems, w_sem):
+    fetch = pltpu.make_async_copy(w_hbm, w_ref, w_sem)
+    fetch.start()
     copies = []
     for i, src in enumerate((k_hbm, v_hbm, q_hbm)):
         for r in range(2):
@@ -42,6 +48,7 @@
                 )
     for copy in copies:
         copy.start()
+    fetch.wait()
     pattern = w_ref[...].astype(jnp.float32)
     pattern = jnp.concatenate([pattern, jnp.zeros((1, 101), jnp.float32)], axis=1)
     row = lax.broadcasted_iota(jnp.int32, (8, 128), 0)
@@ -76,27 +83,35 @@
     return pl.pallas_call(
         pack_kernel,
         out_shape=pltpu.VMEM((16, ROWS // 8, 8, D), jnp.bfloat16),
-        in_specs=[anywhere] * 3 + [VMEM],
+        in_specs=[anywhere] * 4,
         out_specs=VMEM,
         scratch_shapes=[
             pltpu.VMEM((3, 2, COLS, 8, HEADS * D), jnp.bfloat16),
+            pltpu.VMEM((1, 27), jnp.int32),
             pltpu.SemaphoreType.DMA((3, 2, 2)),
+            pltpu.SemaphoreType.DMA,
         ],
         compiler_params=limit(16),
         name="pack",
-    )(*shaped, window.reshape(1, 27))
-
-
-def cut_kernel(all_ref, kv_ref):
-    kv_ref[...] = all_ref[:, 0:KV_ROWS]
+    )(*shaped, pltpu.with_memory_space_constraint(window.reshape(1, 27), pltpu.HBM))
+
+
+def cut_kernel(all_ref, first_ref, last_ref):
+    for part in range(2):
+        row = HALO * 16 * part
+        first_ref[:, FIRST * part : FIRST * (part + 1)] = all_ref[:, row : row + FIRST]
+        last_ref[:, LAST * part : LAST * (part + 1)] = all_ref[:, row + FIRST : row + HALO * 16]
 
 
 def cut(everything):
     return pl.pallas_call(
         cut_kernel,
-        out_shape=pltpu.VMEM((16, KV_ROWS, D), jnp.bfloat16),
+        out_shape=(
+            pltpu.VMEM((16, 2 * FIRST, D), jnp.bfloat16),
+            pltpu.VMEM((16, 2 * LAST, D), jnp.bfloat16),
+        ),
         in_specs=[VMEM],
-        out_specs=VMEM,
+        out_specs=(VMEM, VMEM),
         compiler_params=limit(8),
         name="cut",
     )(resident(everything))
@@ -125,9 +140,9 @@
     return lax.dot_general(q, k, (((1,), (1,)), ((), ())), preferred_element_type=jnp.float32)
 
 
-def weigh(s_ref, slot, refs, oks, shift_from, w, half, total, acc):
-    for n, (ref, b) in enumerate(refs):
-        v = take(ref, (key_index(w, b, half) + HALO) * 16)
+def weigh(s_ref, slot, refs, oks, shift_from, total, acc):
+    for n, value in enumerate(refs):
+        v = value()
         shift = shift_from if oks[n] is None else jnp.where(oks[n], shift_from, BIG)
         p = jnp.exp2(s_ref[slot, :, n * 256 : (n + 1) * 256] * SCALE - shift)
         part = p[:, 0:128] + p[:, 128:256]
@@ -149,7 +164,8 @@
         for ref in (all_ref, mate_ref):
             for b in range(3):
                 n = len(refs)
-                k = take(ref, key_index(w, b, half) * 16)
+                row = key_index(w, b, half) * 16
+                k = take(ref, row)
                 s = scores(q, k)
                 s_ref[slot, :, n * 256 : (n + 1) * 256] = s
                 high = jnp.max(s, axis=1, keepdims=True)
@@ -164,10 +180,10 @@
                     ok = jnp.broadcast_to(mark * gate, (256, 1)) > 0.5
                     high = jnp.where(ok, high, -BIG)
                 top = high if top is None else jnp.maximum(top, high)
-                refs.append((ref, b))
+                refs.append(functools.partial(take, ref, row + HALO * 16))
                 oks.append(ok)
         peak = top * SCALE
-        total, acc = weigh(s_ref, slot, refs, oks, peak, w, half, None, None)
+        total, acc = weigh(s_ref, slot, refs, oks, peak, None, None)
         acc_ref[w] = acc
         total_ref[w] = total
         peak_ref[w] = jnp.broadcast_to(peak, (256, 128))
@@ -196,12 +212,23 @@
     )(resident(everything), resident(mate))
 
 
-def far_kernel(all_ref, far_ref, acc_ref, peak_ref, total_ref, o_ref, s_ref):
+def far_take(first_ref, last_ref, w, b, half, part):
+    spot = w + b - 1
+    index = key_index(w, b, half)
+    early = functools.partial(take, first_ref)
+    if spot < 6:
+        return early(FIRST * part + index * 16)
+    late = functools.partial(take, last_ref)
+    if spot > 6:
+        return late(LAST * part + (index - 7) * 16)
+    return jnp.where(half == 0, early(FIRST * part + 6 * 16), late(LAST * part))
+
+
+def far_kernel(tiles, all_ref, first_ref, last_ref, acc_ref, peak_ref, total_ref, o_ref, s_ref):
     t, half = shard_place()
     even = t % 2 == 0
     t_ok = jnp.where(even, t > 0, t < 7)
-
-    def tile(w, slot):
+    for slot, w in enumerate(tiles):
         column = half * TILES + w
         q = take(all_ref, Q_ROW + 16 * w)
         marks = all_ref[column, pl.ds(MARK_ROW, 8), :].astype(jnp.float32)
@@ -209,44 +236,52 @@
         before = peak_ref[w, :, 0:1]
         top = None
         for b in range(3):
-            k = take(far_ref, key_index(w, b, half) * 16)
-            s = scores(q, k)
+            s = scores(q, far_take(first_ref, last_ref, w, b, half, 0))
             s_ref[slot, :, b * 256 : (b + 1) * 256] = s
             mark = jnp.where(even, marks[b : b + 1, 0:1], marks[5 + b : 6 + b, 0:1])
             gate = jnp.where(columns_ok(column, b) & t_ok, 1.0, 0.0)
             ok = jnp.broadcast_to(mark * gate, (256, 1)) > 0.5
             high = jnp.where(ok, jnp.max(s, axis=1, keepdims=True), -BIG)
             top = high if top is None else jnp.maximum(top, high)
-            refs.append((far_ref, b))
+            refs.append(functools.partial(far_take, first_ref, last_ref, w, b, half, 1))
             oks.append(ok)
         peak = jnp.maximum(before, jnp.where(top > -BIG, top, -BIG / 4) * SCALE)
         fade = jnp.exp2(before - peak)
         total, acc = weigh(
-            s_ref, slot, refs, oks, peak, w, half, total_ref[w] * fade, acc_ref[w] * fade
+            s_ref, slot, refs, oks, peak, total_ref[w] * fade, acc_ref[w] * fade
         )
         out = acc / jnp.sum(total, axis=1, keepdims=True)
-        o_ref[:, pl.ds(pl.multiple_of(16 * w, 16), 16), :] = out.astype(jnp.bfloat16).reshape(
-            16, 16, D
-        )
-
-    def pair(i, carry):
-        tile(2 * i, 0)
-        tile(2 * i + 1, 1)
-        return carry
-
-    lax.fori_loop(0, TILES // 2, pair, 0)
-
-
-def far(everything, other, parts):
+        o_ref[:, 16 * w : 16 * w + 16, :] = out.astype(jnp.bfloat16).reshape(16, 16, D)
+
+
+def far_early_kernel(all_ref, first_ref, acc_ref, peak_ref, total_ref, o_ref, s_ref):
+    far_kernel(
+        range(EARLY), all_ref, first_ref, None, acc_ref, peak_ref, total_ref, o_ref, s_ref
+    )
+
+
+def far_late_kernel(all_ref, first_ref, last_ref, acc_ref, peak_ref, total_ref, _, o_ref, s_ref):
+    far_kernel(
+        range(EARLY, TILES), all_ref, first_ref, last_ref, acc_ref, peak_ref, total_ref, o_ref, s_ref
+    )
+
+
+def far(kernel, name, count, operands, aliases):
     return pl.pallas_call(
-        far_kernel,
+        kernel,
         out_shape=pltpu.VMEM((16, TILES * 16, D), jnp.bfloat16),
-        in_specs=[VMEM] * 5,
+        in_specs=[VMEM] * len(operands),
         out_specs=VMEM,
-        scratch_shapes=[pltpu.VMEM((2, 256, 3 * 256), jnp.float32)],
+        scratch_shapes=[pltpu.VMEM((count, 256, 3 * 256), jnp.float32)],
         compiler_params=limit(16),
-        name="far",
-    )(*[resident(x) for x in (everything, other, *parts)])
+        input_output_aliases=aliases,
+        cost_estimate=pl.CostEstimate(
+            flops=count * 3 * 4 * 256 * 256 * D,
+            bytes_accessed=count << 19,
+            transcendentals=count * 3 * 65536,
+        ),
+        name=name,
+    )(*[resident(x) for x in operands])
 
 
 def unpack_kernel(x_ref, o_ref):
@@ -274,14 +309,24 @@
 
 def body(queries, keys, values, window):
     everything = swap(pack(queries, keys, values, window).reshape(16, ROWS, D))
-    kv = cut(everything)
+    first, last = cut(everything)
     steps = lax.axis_size("temporal")
     across = [(i, i + 1) for i in range(1, steps - 1, 2)]
+    across = across + [(j, i) for i, j in across]
     mates = [(i, i + 1) for i in range(0, steps, 2)]
-    other = lax.ppermute(kv, "temporal", across + [(j, i) for i, j in across])
-    mate = lax.ppermute(kv, "temporal", mates + [(j, i) for i, j in mates])
+    mates = mates + [(j, i) for i, j in mates]
+    far_first = lax.ppermute(first, "temporal", across)
+    far_last = lax.ppermute(last, "temporal", across)
+    mate = lax.ppermute(everything, "temporal", mates)
     parts = near(everything, mate)
-    out = far(everything, other, parts)
+    out = far(far_early_kernel, "far_early", EARLY, (everything, far_first, *parts), {})
+    out = far(
+        far_late_kernel,
+        "far_late",
+        TILES - EARLY,
+        (everything, far_first, far_last, *parts, out),
+        {6: 0},
+    )
     back = swap(out)
     return unpack(back.reshape(16, TILES, 2, 8, D))
 

time: 72.4 us -> 68.8 us (0.950)
  waiting for transfers between devices: 8.82 us -> 2.76 us
  starting transfers between devices: 2.2 us -> 5.57 us
    ppermute x2 -> x3, waiting for transfers between devices: 8.82 us -> 2.76 us  [the longest x1 2.5 us: body(): far_first = lax.ppermute(first, 'temporal', across)]
    ppermute x2 -> x3, starting transfers between devices: 2.2 us -> 5.57 us  [the longest x1 3.43 us: body(): far_last = lax.ppermute(last, 'temporal', across)]
    pallas_call x2 -> x3, Pallas kernels: 4.71 us -> 4.26 us  [the longest x2 4.18 us: far(): pl.pallas_call(kernel, out_shape=pltpu.VMEM((16, TILES * 16, D), jnp.bflo...]
  transfers between devices with their start and end apart: 2 -> 3, of which waited for: 2 -> 2; matrix products, arithmetic and copies ran while one was open for 0% -> 0% of each run, Pallas kernels for 9% -> 13%
where the time goes in v4:
time: 68.8 us; the launch traced here: 68.6 us
  blocking collectives  46.7 us (68%)
  Pallas kernels  13.5 us (20%)
  starting transfers between devices  5.57 us (8%)
  waiting for transfers between devices  2.76 us (4%)
    all_to_all x2, blocking collectives, swap(): return lax.all_to_all(x, 'spatial', split_axis=0, concat_axis=0, tiled=True)  46.7 us
    pallas_call x1, Pallas kernels, near(): pl.pallas_call(near_kernel, out_shape=(part, part, part), in_specs=[VMEM]...  6.61 us
    pallas_call x2, Pallas kernels, far(): pl.pallas_call(kernel, out_shape=pltpu.VMEM((16, TILES * 16, D), jnp.bflo...  4.18 us
    ppermute x1, starting transfers between devices, body(): far_last = lax.ppermute(last, 'temporal', across)  3.43 us
    ppermute x1, waiting for transfers between devices, body(): far_first = lax.ppermute(first, 'temporal', across)  2.5 us
    ppermute x1, starting transfers between devices, body(): far_first = lax.ppermute(first, 'temporal', across)  2.13 us
    pallas_call x1, Pallas kernels, pack(): pl.pallas_call(pack_kernel, out_shape=pltpu.VMEM((16, ROWS // 8, 8, D), j...  1.7 us
  transfers between devices with their start and end apart: 3, of which 2 were waited for; matrix products, arithmetic and copies ran while one was open for 0% of the time, Pallas kernels for 13%

profile of v4, /device:TPU:32, one launch (start us, length us, event | category | flops | bytes accessed | tf_op | source)
XLA Modules:
  0.0 68.6 jit_solution(11960957426498350508)
XLA Ops:
  0.0 1.7 %pack.1 = bf16[16,53,8,128]{3,2,1,0:T(8,128)(2,1)S(1)} custom-call(bf16[2,16,8,1024]{3,2,1,0:T(8,128)(2,1)} %bitcast.9, bf16[2,16,8,1024]{3,2,1,0:T(8,128)(2,1)} %bitcast.10, bf16[2,16,8,1024]{3,2,1,0:T(8,128)(2,1)} %bitcast.11, s32[1,27]{1,0:T(1,128)} %bitcast.12), custom_call_target="tpu_custom_call" | custom-call | tf_op jit(solution)/shard_map/pack/pallas_call | solution.py:83
  1.7 31.4 %all_to_all.10.all_ref = bf16[16,424,128]{2,1,0:T(8,128)(2,1)S(1)} all-to-all(bf16[16,424,128]{2,1,0:T(8,128)(2,1)S(1)} %bitcast.7), channel_id=1, replica_groups=mesh['temporal'=8,'spatial'=16,'head'=2] {'spatial'}, dimensions={0} | all-to-all | bytes 3473408 | tf_op jit(solution)/shard_map/all_to_all | solution.py:307
  33.1 0.0 collective-permute-start.2
  33.1 0.1 cut.1
  33.1 2.1 %collective-permute-start = (bf16[16,224,128]{2,1,0:T(8,128)(2,1)S(1)}, bf16[16,224,128]{2,1,0:T(8,128)(2,1)S(1)}, u32[]{:S(2)}, u32[]{:S(2)}) collective-permute-start(bf16[16,224,128]{2,1,0:T(8,128)(2,1)S(1)} %get-tuple-element.10), channel_id=1, source_target_pairs={{32,64},{96,128},{160,192},{64,32},{128,96},{192,160},{33,65},{97,... | collective-permute-start | bytes 2752520 | tf_op jit(solution)/shard_map/ppermute | solution.py:318
  35.3 3.4 %collective-permute-start.1 = (bf16[16,64,128]{2,1,0:T(8,128)(2,1)S(1)}, bf16[16,64,128]{2,1,0:T(8,128)(2,1)S(1)}, u32[]{:S(2)}, u32[]{:S(2)}) collective-permute-start(bf16[16,64,128]{2,1,0:T(8,128)(2,1)S(1)} %get-tuple-element.11), channel_id=1, source_target_pairs={{32,64},{96,128},{160,192},{64,32},{128,96},{192,160},{33,65},{97,... | collective-permute-start | bytes 786440 | tf_op jit(solution)/shard_map/ppermute | solution.py:319
  38.7 0.0 collective-permute-done.2.mate_ref
  38.7 6.6 %near.1 = (f32[8,256,128]{2,1,0:T(8,128)S(1)}, f32[8,256,128]{2,1,0:T(8,128)S(1)}, f32[8,256,128]{2,1,0:T(8,128)S(1)}) custom-call(bf16[16,424,128]{2,1,0:T(8,128)(2,1)S(1)} %all_to_all.10.all_ref, bf16[16,424,128]{2,1,0:T(8,128)(2,1)S(1)} %collective-permute-done.2.mate_ref), custom_call_target="tpu_custom_call" | custom-call | flops 1610612736 | bytes 6291456 | tf_op jit(solution)/shard_map/near/pallas_call | solution.py:201
  45.4 2.5 %collective-permute-done.first_ref = bf16[16,224,128]{2,1,0:T(8,128)(2,1)S(1)} collective-permute-done((bf16[16,224,128]{2,1,0:T(8,128)(2,1)S(1)}, bf16[16,224,128]{2,1,0:T(8,128)(2,1)S(1)}, u32[]{:S(2)}, u32[]{:S(2)}) %collective-permute-start) | collective-permute-done | bytes 917536 | tf_op jit(solution)/shard_map/ppermute | solution.py:318
  47.9 2.6 %far_early.1._ = bf16[16,128,128]{2,1,0:T(8,128)(2,1)S(1)} custom-call(bf16[16,424,128]{2,1,0:T(8,128)(2,1)S(1)} %all_to_all.10.all_ref, bf16[16,224,128]{2,1,0:T(8,128)(2,1)S(1)} %collective-permute-done.first_ref, f32[8,256,128]{2,1,0:T(8,128)S(1)} %get-tuple-element.12.acc_ref, f32[8,256,128]{2,1,0:T(8,128)S(1)} %get-tuple-element.13.peak_ref, ...), custom_call_target="tpu_custom_call" | custom-call | flops 503316480 | bytes 2621440 | tf_op jit(solution)/shard_map/far_early/pallas_call | solution.py:270
  50.4 0.3 collective-permute-done.1.last_ref
  50.7 1.6 %far_late.1 = bf16[16,128,128]{2,1,0:T(8,128)(2,1)S(1)} custom-call(bf16[16,424,128]{2,1,0:T(8,128)(2,1)S(1)} %all_to_all.10.all_ref, bf16[16,224,128]{2,1,0:T(8,128)(2,1)S(1)} %collective-permute-done.first_ref, bf16[16,64,128]{2,1,0:T(8,128)(2,1)S(1)} %collective-permute-done.1.last_ref, ...), custom_call_target="tpu_custom_call", output_to_operand_aliasing={{}: (6, {})} | custom-call | flops 301989888 | bytes 1572864 | tf_op jit(solution)/shard_map/far_late/pallas_call | solution.py:270
  52.3 15.3 %all_to_all.11 = bf16[16,128,128]{2,1,0:T(8,128)(2,1)S(1)} all-to-all(bf16[16,128,128]{2,1,0:T(8,128)(2,1)S(1)} %far_late.1), channel_id=1, replica_groups=mesh['temporal'=8,'spatial'=16,'head'=2] {'spatial'}, dimensions={0} | all-to-all | bytes 1048576 | tf_op jit(solution)/shard_map/all_to_all | solution.py:307
  67.6 0.9 %unpack.1 = bf16[2,16,8,1024]{3,2,1,0:T(8,128)(2,1)} custom-call(bf16[16,8,2,8,128]{4,3,2,1,0:T(8,128)(2,1)S(1)} %bitcast.8), custom_call_target="tpu_custom_call" | custom-call | tf_op jit(solution)/shard_map/unpack/pallas_call | solution.py:295
Async XLA Ops:
  33.1 5.7 %collective-permute-start.2 = (bf16[16,424,128]{2,1,0:T(8,128)(2,1)S(1)}, bf16[16,424,128]{2,1,0:T(8,128)(2,1)S(1)}, u32[]{:S(2)}, u32[]{:S(2)}) collective-permute-start(bf16[16,424,128]{2,1,0:T(8,128)(2,1)S(1)} %all_to_all.10.all_ref), channel_id=1, source_target_pairs={{0,32},{64,96},{128,160},{192,224},{32,0},{96,64},{160,128},{224,1... | collective-permute-start | bytes 5210120 | tf_op jit(solution)/shard_map/ppermute | solution.py:320
  33.1 14.7 %collective-permute-start = (bf16[16,224,128]{2,1,0:T(8,128)(2,1)S(1)}, bf16[16,224,128]{2,1,0:T(8,128)(2,1)S(1)}, u32[]{:S(2)}, u32[]{:S(2)}) collective-permute-start(bf16[16,224,128]{2,1,0:T(8,128)(2,1)S(1)} %get-tuple-element.10), channel_id=1, source_target_pairs={{32,64},{96,128},{160,192},{64,32},{128,96},{192,160},{33,65},{97,... | collective-permute-start | bytes 2752520 | tf_op jit(solution)/shard_map/ppermute | solution.py:318
  35.3 15.4 %collective-permute-start.1 = (bf16[16,64,128]{2,1,0:T(8,128)(2,1)S(1)}, bf16[16,64,128]{2,1,0:T(8,128)(2,1)S(1)}, u32[]{:S(2)}, u32[]{:S(2)}) collective-permute-start(bf16[16,64,128]{2,1,0:T(8,128)(2,1)S(1)} %get-tuple-element.11), channel_id=1, source_target_pairs={{32,64},{96,128},{160,192},{64,32},{128,96},{192,160},{33,65},{97,... | collective-permute-start | bytes 786440 | tf_op jit(solution)/shard_map/ppermute | solution.py:319

commit v5 on v4

--- a/solution.py
+++ b/solution.py
@@ -266,7 +266,7 @@
     )
 
 
-def far(kernel, name, count, operands, aliases):
+def far(kernel, count, operands, aliases):
     return pl.pallas_call(
         kernel,
         out_shape=pltpu.VMEM((16, TILES * 16, D), jnp.bfloat16),
@@ -280,23 +280,33 @@
             bytes_accessed=count << 19,
             transcendentals=count * 3 * 65536,
         ),
-        name=name,
     )(*[resident(x) for x in operands])
 
 
-def unpack_kernel(x_ref, o_ref):
-    for h in range(HEADS):
+def unpack_kernel(x_ref, o_hbm, buf, sems):
+    copies = []
+    for r in range(2):
         for half in range(2):
-            for r in range(2):
-                o_ref[r, pl.ds(8 * half, TILES), :, pl.ds(h * D, D)] = x_ref[2 * h + half, :, r]
+            cut_out = pl.ds(8 * half, TILES)
+            for h in range(HEADS):
+                buf[r, cut_out, :, pl.ds(h * D, D)] = x_ref[2 * h + half, :, r]
+            copy = pltpu.make_async_copy(
+                buf.at[r, cut_out], o_hbm.at[r, cut_out], sems.at[r, half]
+            )
+            copy.start()
+            copies.append(copy)
+    for copy in copies:
+        copy.wait()
 
 
 def unpack(x):
+    shape = (2, COLS, 8, HEADS * D)
     out = pl.pallas_call(
         unpack_kernel,
-        out_shape=jax.ShapeDtypeStruct((2, COLS, 8, HEADS * D), jnp.bfloat16),
+        out_shape=jax.ShapeDtypeStruct(shape, jnp.bfloat16),
         in_specs=[VMEM],
-        out_specs=VMEM,
+        out_specs=pl.BlockSpec(memory_space=pl.ANY),
+        scratch_shapes=[pltpu.VMEM(shape, jnp.bfloat16), pltpu.SemaphoreType.DMA((2, 2))],
         compiler_params=limit(8),
         name="unpack",
     )(resident(x))
@@ -316,16 +326,12 @@
     mates = [(i, i + 1) for i in range(0, steps, 2)]
     mates = mates + [(j, i) for i, j in mates]
     far_first = lax.ppermute(first, "temporal", across)
+    mate = lax.ppermute(everything, "temporal", mates)
     far_last = lax.ppermute(last, "temporal", across)
-    mate = lax.ppermute(everything, "temporal", mates)
     parts = near(everything, mate)
-    out = far(far_early_kernel, "far_early", EARLY, (everything, far_first, *parts), {})
+    out = far(far_early_kernel, EARLY, (everything, far_first, *parts), {})
     out = far(
-        far_late_kernel,
-        "far_late",
-        TILES - EARLY,
-        (everything, far_first, far_last, *parts, out),
-        {6: 0},
+        far_late_kernel, TILES - EARLY, (everything, far_first, far_last, *parts, out), {6: 0}
     )
     back = swap(out)
     return unpack(back.reshape(16, TILES, 2, 8, D))

time: 68.8 us -> 68.7 us (level)
  no operation moved by 1% of the time
where the time goes in v5:
time: 68.7 us; the launch traced here: 68.5 us
  blocking collectives  46.7 us (68%)
  Pallas kernels  13.4 us (20%)
  starting transfers between devices  5.57 us (8%)
  waiting for transfers between devices  2.76 us (4%)
    all_to_all x2, blocking collectives, swap(): return lax.all_to_all(x, 'spatial', split_axis=0, concat_axis=0, tiled=True)  46.7 us
    pallas_call x1, Pallas kernels, near(): pl.pallas_call(near_kernel, out_shape=(part, part, part), in_specs=[VMEM]...  6.61 us
    pallas_call x2, Pallas kernels, far(): pl.pallas_call(kernel, out_shape=pltpu.VMEM((16, TILES * 16, D), jnp.bflo...  4.18 us
    ppermute x1, starting transfers between devices, body(): far_last = lax.ppermute(last, 'temporal', across)  3.43 us
    ppermute x1, waiting for transfers between devices, body(): far_first = lax.ppermute(first, 'temporal', across)  2.5 us
    ppermute x1, starting transfers between devices, body(): far_first = lax.ppermute(first, 'temporal', across)  2.13 us
    pallas_call x1, Pallas kernels, pack(): pl.pallas_call(pack_kernel, out_shape=pltpu.VMEM((16, ROWS // 8, 8, D), j...  1.7 us
  transfers between devices with their start and end apart: 3, of which 2 were waited for; matrix products, arithmetic and copies ran while one was open for 0% of the time, Pallas kernels for 13%

profile of v5, /device:TPU:32, one launch (start us, length us, event | category | flops | bytes accessed | tf_op | source)
XLA Modules:
  0.0 68.5 jit_solution(6760215088399095445)
XLA Ops:
  0.0 1.7 %pack.1 = bf16[16,53,8,128]{3,2,1,0:T(8,128)(2,1)S(1)} custom-call(bf16[2,16,8,1024]{3,2,1,0:T(8,128)(2,1)} %bitcast.9, bf16[2,16,8,1024]{3,2,1,0:T(8,128)(2,1)} %bitcast.10, bf16[2,16,8,1024]{3,2,1,0:T(8,128)(2,1)} %bitcast.11, s32[1,27]{1,0:T(1,128)} %bitcast.12), custom_call_target="tpu_custom_call" | custom-call | tf_op jit(solution)/shard_map/pack/pallas_call | solution.py:83
  1.7 31.4 %all_to_all.10.all_ref = bf16[16,424,128]{2,1,0:T(8,128)(2,1)S(1)} all-to-all(bf16[16,424,128]{2,1,0:T(8,128)(2,1)S(1)} %bitcast.7), channel_id=1, replica_groups=mesh['temporal'=8,'spatial'=16,'head'=2] {'spatial'}, dimensions={0} | all-to-all | bytes 3473408 | tf_op jit(solution)/shard_map/all_to_all | solution.py:317
  33.1 0.0 collective-permute-start.2
  33.1 0.1 cut.1
  33.1 2.1 %collective-permute-start = (bf16[16,224,128]{2,1,0:T(8,128)(2,1)S(1)}, bf16[16,224,128]{2,1,0:T(8,128)(2,1)S(1)}, u32[]{:S(2)}, u32[]{:S(2)}) collective-permute-start(bf16[16,224,128]{2,1,0:T(8,128)(2,1)S(1)} %get-tuple-element.10), channel_id=1, source_target_pairs={{32,64},{96,128},{160,192},{64,32},{128,96},{192,160},{33,65},{97,... | collective-permute-start | bytes 2752520 | tf_op jit(solution)/shard_map/ppermute | solution.py:328
  35.3 3.4 %collective-permute-start.1 = (bf16[16,64,128]{2,1,0:T(8,128)(2,1)S(1)}, bf16[16,64,128]{2,1,0:T(8,128)(2,1)S(1)}, u32[]{:S(2)}, u32[]{:S(2)}) collective-permute-start(bf16[16,64,128]{2,1,0:T(8,128)(2,1)S(1)} %get-tuple-element.11), channel_id=1, source_target_pairs={{32,64},{96,128},{160,192},{64,32},{128,96},{192,160},{33,65},{97,... | collective-permute-start | bytes 786440 | tf_op jit(solution)/shard_map/ppermute | solution.py:330
  38.7 0.0 collective-permute-done.2.mate_ref
  38.7 6.6 %near.1 = (f32[8,256,128]{2,1,0:T(8,128)S(1)}, f32[8,256,128]{2,1,0:T(8,128)S(1)}, f32[8,256,128]{2,1,0:T(8,128)S(1)}) custom-call(bf16[16,424,128]{2,1,0:T(8,128)(2,1)S(1)} %all_to_all.10.all_ref, bf16[16,424,128]{2,1,0:T(8,128)(2,1)S(1)} %collective-permute-done.2.mate_ref), custom_call_target="tpu_custom_call" | custom-call | flops 1610612736 | bytes 6291456 | tf_op jit(solution)/shard_map/near/pallas_call | solution.py:201
  45.4 2.5 %collective-permute-done.first_ref = bf16[16,224,128]{2,1,0:T(8,128)(2,1)S(1)} collective-permute-done((bf16[16,224,128]{2,1,0:T(8,128)(2,1)S(1)}, bf16[16,224,128]{2,1,0:T(8,128)(2,1)S(1)}, u32[]{:S(2)}, u32[]{:S(2)}) %collective-permute-start) | collective-permute-done | bytes 917536 | tf_op jit(solution)/shard_map/ppermute | solution.py:328
  47.9 2.6 %shard_map.46._ = bf16[16,128,128]{2,1,0:T(8,128)(2,1)S(1)} custom-call(bf16[16,424,128]{2,1,0:T(8,128)(2,1)S(1)} %all_to_all.10.all_ref, bf16[16,224,128]{2,1,0:T(8,128)(2,1)S(1)} %collective-permute-done.first_ref, f32[8,256,128]{2,1,0:T(8,128)S(1)} %get-tuple-element.12.acc_ref, f32[8,256,128]{2,1,0:T(8,128)S(1)} %get-tuple-element.13.peak_ref, ...), custom_call_target="tpu_custom_call" | custom-call | flops 503316480 | bytes 2621440 | tf_op jit(solution)/shard_map/pallas_call | solution.py:270
  50.4 0.3 collective-permute-done.1.last_ref
  50.7 1.6 %shard_map.47 = bf16[16,128,128]{2,1,0:T(8,128)(2,1)S(1)} custom-call(bf16[16,424,128]{2,1,0:T(8,128)(2,1)S(1)} %all_to_all.10.all_ref, bf16[16,224,128]{2,1,0:T(8,128)(2,1)S(1)} %collective-permute-done.first_ref, bf16[16,64,128]{2,1,0:T(8,128)(2,1)S(1)} %collective-permute-done.1.last_ref, ...), custom_call_target="tpu_custom_call", output_to_operand_aliasing={{}: (6, {})} | custom-call | flops 301989888 | bytes 1572864 | tf_op jit(solution)/shard_map/pallas_call | solution.py:270
  52.3 15.3 %all_to_all.11 = bf16[16,128,128]{2,1,0:T(8,128)(2,1)S(1)} all-to-all(bf16[16,128,128]{2,1,0:T(8,128)(2,1)S(1)} %shard_map.47), channel_id=1, replica_groups=mesh['temporal'=8,'spatial'=16,'head'=2] {'spatial'}, dimensions={0} | all-to-all | bytes 1048576 | tf_op jit(solution)/shard_map/all_to_all | solution.py:317
  67.6 0.8 %unpack.1 = bf16[2,16,8,1024]{3,2,1,0:T(8,128)(2,1)} custom-call(bf16[16,8,2,8,128]{4,3,2,1,0:T(8,128)(2,1)S(1)} %bitcast.8), custom_call_target="tpu_custom_call" | custom-call | tf_op jit(solution)/shard_map/unpack/pallas_call | solution.py:304
Async XLA Ops:
  33.1 5.7 %collective-permute-start.2 = (bf16[16,424,128]{2,1,0:T(8,128)(2,1)S(1)}, bf16[16,424,128]{2,1,0:T(8,128)(2,1)S(1)}, u32[]{:S(2)}, u32[]{:S(2)}) collective-permute-start(bf16[16,424,128]{2,1,0:T(8,128)(2,1)S(1)} %all_to_all.10.all_ref), channel_id=1, source_target_pairs={{0,32},{64,96},{128,160},{192,224},{32,0},{96,64},{160,128},{224,1... | collective-permute-start | bytes 5210120 | tf_op jit(solution)/shard_map/ppermute | solution.py:329
  33.1 14.7 %collective-permute-start = (bf16[16,224,128]{2,1,0:T(8,128)(2,1)S(1)}, bf16[16,224,128]{2,1,0:T(8,128)(2,1)S(1)}, u32[]{:S(2)}, u32[]{:S(2)}) collective-permute-start(bf16[16,224,128]{2,1,0:T(8,128)(2,1)S(1)} %get-tuple-element.10), channel_id=1, source_target_pairs={{32,64},{96,128},{160,192},{64,32},{128,96},{192,160},{33,65},{97,... | collective-permute-start | bytes 2752520 | tf_op jit(solution)/shard_map/ppermute | solution.py:328
  35.3 15.4 %collective-permute-start.1 = (bf16[16,64,128]{2,1,0:T(8,128)(2,1)S(1)}, bf16[16,64,128]{2,1,0:T(8,128)(2,1)S(1)}, u32[]{:S(2)}, u32[]{:S(2)}) collective-permute-start(bf16[16,64,128]{2,1,0:T(8,128)(2,1)S(1)} %get-tuple-element.11), channel_id=1, source_target_pairs={{32,64},{96,128},{160,192},{64,32},{128,96},{192,160},{33,65},{97,... | collective-permute-start | bytes 786440 | tf_op jit(solution)/shard_map/ppermute | solution.py:330

commit v6 on v5

--- a/solution.py
+++ b/solution.py
@@ -96,7 +96,8 @@
     )(*shaped, pltpu.with_memory_space_constraint(window.reshape(1, 27), pltpu.HBM))
 
 
-def cut_kernel(all_ref, first_ref, last_ref):
+def cut_kernel(all_ref, first_ref, last_ref, both_ref):
+    both_ref[...] = all_ref[:, 0:KV_ROWS]
     for part in range(2):
         row = HALO * 16 * part
         first_ref[:, FIRST * part : FIRST * (part + 1)] = all_ref[:, row : row + FIRST]
@@ -109,9 +110,10 @@
         out_shape=(
             pltpu.VMEM((16, 2 * FIRST, D), jnp.bfloat16),
             pltpu.VMEM((16, 2 * LAST, D), jnp.bfloat16),
+            pltpu.VMEM((16, KV_ROWS, D), jnp.bfloat16),
         ),
         in_specs=[VMEM],
-        out_specs=(VMEM, VMEM),
+        out_specs=(VMEM,) * 3,
         compiler_params=limit(8),
         name="cut",
     )(resident(everything))
@@ -319,14 +321,14 @@
 
 def body(queries, keys, values, window):
     everything = swap(pack(queries, keys, values, window).reshape(16, ROWS, D))
-    first, last = cut(everything)
+    first, last, both = cut(everything)
     steps = lax.axis_size("temporal")
     across = [(i, i + 1) for i in range(1, steps - 1, 2)]
     across = across + [(j, i) for i, j in across]
     mates = [(i, i + 1) for i in range(0, steps, 2)]
     mates = mates + [(j, i) for i, j in mates]
     far_first = lax.ppermute(first, "temporal", across)
-    mate = lax.ppermute(everything, "temporal", mates)
+    mate = lax.ppermute(both, "temporal", mates)
     far_last = lax.ppermute(last, "temporal", across)
     parts = near(everything, mate)
     out = far(far_early_kernel, EARLY, (everything, far_first, *parts), {})

time: 68.7 us -> 68.8 us (level)
  no operation moved by 1% of the time
where the time goes in v6:
time: 68.8 us; the launch traced here: 68.6 us
  blocking collectives  46.6 us (68%)
  Pallas kernels  13.5 us (20%)
  starting transfers between devices  5.66 us (8%)
  waiting for transfers between devices  2.76 us (4%)
    all_to_all x2, blocking collectives, swap(): return lax.all_to_all(x, 'spatial', split_axis=0, concat_axis=0, tiled=True)  46.6 us
    pallas_call x1, Pallas kernels, near(): pl.pallas_call(near_kernel, out_shape=(part, part, part), in_specs=[VMEM]...  6.61 us
    pallas_call x2, Pallas kernels, far(): pl.pallas_call(kernel, out_shape=pltpu.VMEM((16, TILES * 16, D), jnp.bflo...  4.18 us
    ppermute x1, starting transfers between devices, body(): far_last = lax.ppermute(last, 'temporal', across)  3.46 us
    ppermute x1, waiting for transfers between devices, body(): far_first = lax.ppermute(first, 'temporal', across)  2.51 us
    ppermute x1, starting transfers between devices, body(): far_first = lax.ppermute(first, 'temporal', across)  2.11 us
    pallas_call x1, Pallas kernels, pack(): pl.pallas_call(pack_kernel, out_shape=pltpu.VMEM((16, ROWS // 8, 8, D), j...  1.7 us
  transfers between devices with their start and end apart: 3, of which 2 were waited for; matrix products, arithmetic and copies ran while one was open for 0% of the time, Pallas kernels for 13%

profile of v6, /device:TPU:32, one launch (start us, length us, event | category | flops | bytes accessed | tf_op | source)
XLA Modules:
  0.0 68.6 jit_solution(9571058117408164499)
XLA Ops:
  0.0 1.7 %pack.1 = bf16[16,53,8,128]{3,2,1,0:T(8,128)(2,1)S(1)} custom-call(bf16[2,16,8,1024]{3,2,1,0:T(8,128)(2,1)} %bitcast.9, bf16[2,16,8,1024]{3,2,1,0:T(8,128)(2,1)} %bitcast.10, bf16[2,16,8,1024]{3,2,1,0:T(8,128)(2,1)} %bitcast.11, s32[1,27]{1,0:T(1,128)} %bitcast.12), custom_call_target="tpu_custom_call" | custom-call | tf_op jit(solution)/shard_map/pack/pallas_call | solution.py:83
  1.7 31.4 %all_to_all.10.all_ref = bf16[16,424,128]{2,1,0:T(8,128)(2,1)S(1)} all-to-all(bf16[16,424,128]{2,1,0:T(8,128)(2,1)S(1)} %bitcast.7), channel_id=1, replica_groups=mesh['temporal'=8,'spatial'=16,'head'=2] {'spatial'}, dimensions={0} | all-to-all | bytes 3473408 | tf_op jit(solution)/shard_map/all_to_all | solution.py:319
  33.1 0.2 cut.1
  33.2 0.1 collective-permute-start.2
  33.3 2.1 %collective-permute-start = (bf16[16,224,128]{2,1,0:T(8,128)(2,1)S(1)}, bf16[16,224,128]{2,1,0:T(8,128)(2,1)S(1)}, u32[]{:S(2)}, u32[]{:S(2)}) collective-permute-start(bf16[16,224,128]{2,1,0:T(8,128)(2,1)S(1)} %get-tuple-element.11), channel_id=1, source_target_pairs={{32,64},{96,128},{160,192},{64,32},{128,96},{192,160},{33,65},{97,... | collective-permute-start | bytes 2752520 | tf_op jit(solution)/shard_map/ppermute | solution.py:330
  35.4 3.5 %collective-permute-start.1 = (bf16[16,64,128]{2,1,0:T(8,128)(2,1)S(1)}, bf16[16,64,128]{2,1,0:T(8,128)(2,1)S(1)}, u32[]{:S(2)}, u32[]{:S(2)}) collective-permute-start(bf16[16,64,128]{2,1,0:T(8,128)(2,1)S(1)} %get-tuple-element.12), channel_id=1, source_target_pairs={{32,64},{96,128},{160,192},{64,32},{128,96},{192,160},{33,65},{97,... | collective-permute-start | bytes 786440 | tf_op jit(solution)/shard_map/ppermute | solution.py:332
  38.9 0.0 collective-permute-done.2.mate_ref
  38.9 6.6 %near.1 = (f32[8,256,128]{2,1,0:T(8,128)S(1)}, f32[8,256,128]{2,1,0:T(8,128)S(1)}, f32[8,256,128]{2,1,0:T(8,128)S(1)}) custom-call(bf16[16,424,128]{2,1,0:T(8,128)(2,1)S(1)} %all_to_all.10.all_ref, bf16[16,288,128]{2,1,0:T(8,128)(2,1)S(1)} %collective-permute-done.2.mate_ref), custom_call_target="tpu_custom_call" | custom-call | flops 1610612736 | bytes 6291456 | tf_op jit(solution)/shard_map/near/pallas_call | solution.py:203
  45.5 2.5 %collective-permute-done.first_ref = bf16[16,224,128]{2,1,0:T(8,128)(2,1)S(1)} collective-permute-done((bf16[16,224,128]{2,1,0:T(8,128)(2,1)S(1)}, bf16[16,224,128]{2,1,0:T(8,128)(2,1)S(1)}, u32[]{:S(2)}, u32[]{:S(2)}) %collective-permute-start) | collective-permute-done | bytes 917536 | tf_op jit(solution)/shard_map/ppermute | solution.py:330
  48.0 2.6 %shard_map.46._ = bf16[16,128,128]{2,1,0:T(8,128)(2,1)S(1)} custom-call(bf16[16,424,128]{2,1,0:T(8,128)(2,1)S(1)} %all_to_all.10.all_ref, bf16[16,224,128]{2,1,0:T(8,128)(2,1)S(1)} %collective-permute-done.first_ref, f32[8,256,128]{2,1,0:T(8,128)S(1)} %get-tuple-element.14.acc_ref, f32[8,256,128]{2,1,0:T(8,128)S(1)} %get-tuple-element.15.peak_ref, ...), custom_call_target="tpu_custom_call" | custom-call | flops 503316480 | bytes 2621440 | tf_op jit(solution)/shard_map/pallas_call | solution.py:272
  50.6 0.3 collective-permute-done.1.last_ref
  50.8 1.6 %shard_map.47 = bf16[16,128,128]{2,1,0:T(8,128)(2,1)S(1)} custom-call(bf16[16,424,128]{2,1,0:T(8,128)(2,1)S(1)} %all_to_all.10.all_ref, bf16[16,224,128]{2,1,0:T(8,128)(2,1)S(1)} %collective-permute-done.first_ref, bf16[16,64,128]{2,1,0:T(8,128)(2,1)S(1)} %collective-permute-done.1.last_ref, ...), custom_call_target="tpu_custom_call", output_to_operand_aliasing={{}: (6, {})} | custom-call | flops 301989888 | bytes 1572864 | tf_op jit(solution)/shard_map/pallas_call | solution.py:272
  52.5 15.3 %all_to_all.11 = bf16[16,128,128]{2,1,0:T(8,128)(2,1)S(1)} all-to-all(bf16[16,128,128]{2,1,0:T(8,128)(2,1)S(1)} %shard_map.47), channel_id=1, replica_groups=mesh['temporal'=8,'spatial'=16,'head'=2] {'spatial'}, dimensions={0} | all-to-all | bytes 1048576 | tf_op jit(solution)/shard_map/all_to_all | solution.py:319
  67.8 0.8 %unpack.1 = bf16[2,16,8,1024]{3,2,1,0:T(8,128)(2,1)} custom-call(bf16[16,8,2,8,128]{4,3,2,1,0:T(8,128)(2,1)S(1)} %bitcast.8), custom_call_target="tpu_custom_call" | custom-call | tf_op jit(solution)/shard_map/unpack/pallas_call | solution.py:306
Async XLA Ops:
  33.2 5.7 %collective-permute-start.2 = (bf16[16,288,128]{2,1,0:T(8,128)(2,1)S(1)}, bf16[16,288,128]{2,1,0:T(8,128)(2,1)S(1)}, u32[]{:S(2)}, u32[]{:S(2)}) collective-permute-start(bf16[16,288,128]{2,1,0:T(8,128)(2,1)S(1)} %get-tuple-element.13), channel_id=1, source_target_pairs={{0,32},{64,96},{128,160},{192,224},{32,0},{96,64},{160,128},{224,1... | collective-permute-start | bytes 3538952 | tf_op jit(solution)/shard_map/ppermute | solution.py:331
  33.3 14.7 %collective-permute-start = (bf16[16,224,128]{2,1,0:T(8,128)(2,1)S(1)}, bf16[16,224,128]{2,1,0:T(8,128)(2,1)S(1)}, u32[]{:S(2)}, u32[]{:S(2)}) collective-permute-start(bf16[16,224,128]{2,1,0:T(8,128)(2,1)S(1)} %get-tuple-element.11), channel_id=1, source_target_pairs={{32,64},{96,128},{160,192},{64,32},{128,96},{192,160},{33,65},{97,... | collective-permute-start | bytes 2752520 | tf_op jit(solution)/shard_map/ppermute | solution.py:330
  35.4 15.4 %collective-permute-start.1 = (bf16[16,64,128]{2,1,0:T(8,128)(2,1)S(1)}, bf16[16,64,128]{2,1,0:T(8,128)(2,1)S(1)}, u32[]{:S(2)}, u32[]{:S(2)}) collective-permute-start(bf16[16,64,128]{2,1,0:T(8,128)(2,1)S(1)} %get-tuple-element.12), channel_id=1, source_target_pairs={{32,64},{96,128},{160,192},{64,32},{128,96},{192,160},{33,65},{97,... | collective-permute-start | bytes 786440 | tf_op jit(solution)/shard_map/ppermute | solution.py:332
